TPU v7x, 32 devices: a whole 2x2x4 slice. The times are simulated.
32 devices in a mesh: ctx: 8 (over z, x), wsh: 4 (over y, core).
Axes of the slice: x: 2, y: 2, z: 4, core: 2. Of those that a mesh axis runs over, the one named last changes fastest.
Arguments:
- inputs: bfloat16 [8, 1024, 768], P('wsh', 'ctx'), may hold values from -6 to 6
- teacher: bfloat16 [8, 1024, 768], P('wsh', 'ctx'), may hold values from -6 to 6
- seq_lengths: int32 [8], P('wsh'), may hold values from 256 to 1024, as said below
- gain_attn: bfloat16 [768], P('wsh'), may hold values from 0.5 to 1.5
- w_query: bfloat16 [768, 768], P('wsh'), may hold values from -0.109375 to 0.109375
- w_key: bfloat16 [768, 768], P('wsh'), may hold values from -0.109375 to 0.109375
- w_value: bfloat16 [768, 768], P('wsh'), may hold values from -0.21875 to 0.21875
- w_out: bfloat16 [768, 768], P('wsh'), may hold values from -2.5 to 2.5
- bias_table: bfloat16 [32, 12], P('wsh'), may hold values from -4 to 4
- gain_ffn: bfloat16 [768], P('wsh'), may hold values from 0.5 to 1.5
- w_inner: bfloat16 [768, 3072], P('wsh'), may hold values from -0.21875 to 0.21875
- w_outer: bfloat16 [3072, 768], P('wsh'), may hold values from -0.109375 to 0.109375
Outputs:
- layer_out: bfloat16 [8, 1024, 768], P('wsh', 'ctx')
- loss_value: float32 [], replicated
- input_grad: float32 [8, 1024, 768], P('wsh', 'ctx')
- gain_attn_grad: float32 [768], P('wsh')
- w_query_grad: float32 [768, 768], P('wsh')
- w_key_grad: float32 [768, 768], P('wsh')
- w_value_grad: float32 [768, 768], P('wsh')
- w_out_grad: float32 [768, 768], P('wsh')
- bias_table_grad: float32 [32, 12], P('wsh')
- gain_ffn_grad: float32 [768], P('wsh')
- w_inner_grad: float32 [768, 3072], P('wsh')
- w_outer_grad: float32 [3072, 768], P('wsh')
Inputs may be any that keep to these rules, and one draw needn't show every extreme that they name: `seq_lengths`: in each aligned group of 2 sequences exactly one, chosen by the seed, has all 1024 tokens valid; every other sequence has fewer.
All inputs are finite; a program needn't handle non-finite values.
Results may differ from a plain program's by a relative error of at most 0.017.
Values may be sent and summed in bfloat16 or wider, within the bound.
No kernel may reach another device: no remote copies, remote signals or barrier semaphores. Data moves between devices by JAX's collectives and lax.ppermute only.
A program may use at most 128 MiB of HBM per device.

v0:
```python
import functools

import jax
import jax.numpy as jnp
from jax import lax
from jax.experimental import pallas as pl
from jax.experimental.pallas import tpu as pltpu
from jax.sharding import PartitionSpec as P

D = 768
H = 12
DH = 64
BUCKETS = 32
SEQ_DEV = 2
PIECE = 128
TP = 4
HEADS = H // TP
COLS = HEADS * DH
OWN = D // TP
ROWS = SEQ_DEV * PIECE
GROUP = ROWS * TP
DEPTH = OWN // 8
START_MIB = 60
EPS = 1e-06
NEG_FILL = -1e30
BUCKET_EDGES = (12, 16, 23, 32, 46, 64, 91)
AXES = ("ctx", "wsh")
ORDER = (0, 2, 1, 3)

ME, X, Z, SEQ_OWNER, SEQ_BIT, QUERY_BLOCKS = range(6)
KEY_BLOCKS = QUERY_BLOCKS + 8

BF16 = jnp.bfloat16
F32 = jnp.float32
NT = (((1,), (1,)), ((), ()))
TN = (((0,), (0,)), ((), ()))
NN = (((1,), (0,)), ((), ()))


def dot(left, right, dims=NN):
    return lax.dot_general(left, right, dims, preferred_element_type=F32)


def swapped(index):
    return (index & 1) * 2 + (index >> 1)


def seq_routes(n_ctx):
    spread = n_ctx // (SEQ_DEV * TP)
    same, cross = [], []
    for c in range(n_ctx):
        for w in range(TP):
            pair = c // 2
            for b in range(2):
                home = (2 * swapped(w) + b) * spread + pair // TP
                route = (c * TP + w, home * TP + swapped(pair % TP))
                (same if b == c % 2 else cross).append(route)
    return same, cross


def backwards(routes):
    return [(there, here) for here, there in routes]


def to_partner(value, offset):
    return lax.ppermute(value, "wsh", [(i, i ^ offset) for i in range(TP)])


def to_ctx(value, offset):
    n_ctx = lax.axis_size("ctx")
    return lax.ppermute(value, "ctx", [(i, i ^ offset) for i in range(n_ctx)])


def swap_blocks(blocks, axis, groups=None):
    return lax.all_to_all(blocks, axis, 0, 0, tiled=True, axis_index_groups=groups)


def pick(stack, index):
    return lax.dynamic_index_in_dim(stack, index, 0, keepdims=False)


def after(value, *earlier):
    return lax.optimization_barrier((value,) + earlier)[0]


def bucket_index(offset):
    distance = jnp.abs(offset)
    far_bucket = 8 + sum(((distance >= edge).astype(jnp.int32) for edge in BUCKET_EDGES))
    near_or_far = jnp.where(distance < 8, distance, far_bucket)
    return near_or_far + jnp.where(offset > 0, 16, 0)


def gelu_and_slope(values):
    cumulative = 0.5 * (1.0 + lax.erf(values * 0.7071067811865476))
    density = jnp.exp(-0.5 * values * values) * 0.3989422804014327
    return values * cumulative, cumulative + values * density


def inverse_rms(values):
    return lax.rsqrt(jnp.mean(values * values, axis=-1, keepdims=True) + EPS)


def norm_back(values, gain, grad):
    scale = inverse_rms(values)
    unit = values * scale
    scaled = gain * grad
    back = scale * (scaled - unit * jnp.mean(scaled * unit, axis=-1, keepdims=True))
    return back, jnp.sum(grad * unit, axis=0, keepdims=True)


def repeat(count, unroll, body, carry):
    if unroll:
        for index in range(count):
            carry = body(index, carry)
        return carry
    return lax.fori_loop(0, count, body, carry)


def vmem():
    return pl.BlockSpec(memory_space=pltpu.VMEM)


def smem():
    return pl.BlockSpec(memory_space=pltpu.SMEM)


def shape(*dims, dtype=F32):
    return jax.ShapeDtypeStruct(dims, dtype)


def hbm():
    return pl.BlockSpec(memory_space=pl.ANY)


def name_of(body):
    return (body.func if isinstance(body, functools.partial) else body).__name__


def run(here, *jobs, scratch=(), mib=10, weight=1):
    args = [a for _, _, given in jobs for a in given]
    outs = [o for _, made, _ in jobs for o in made]

    def bodies(here, *refs):
        ins, rest = refs[: len(args)], refs[len(args) :]
        made, extra = rest[: len(outs)], rest[len(outs) :]
        i = o = 0
        for body, shapes, given in jobs:
            body(here, *ins[i : i + len(given)], *made[o : o + len(shapes)], *extra)
            i, o = i + len(given), o + len(shapes)

    bodies.__name__ = "_".join(name_of(body) for body, _, _ in jobs)
    results = list(call(bodies, outs, [here] + args, scratch, mib, weight=weight))
    return [tuple(results.pop(0) for _ in made) for _, made, _ in jobs]


def call(body, outs, args, scratch=(), mib=10, in_hbm=0, weight=1):
    return pl.pallas_call(
        body,
        name=name_of(body),
        out_shape=tuple(outs),
        in_specs=[smem()] + [hbm()] * in_hbm + [vmem()] * (len(args) - 1 - in_hbm),
        out_specs=(vmem(),) * len(outs),
        scratch_shapes=tuple(scratch),
        compiler_params=pltpu.CompilerParams(vmem_limit_bytes=mib * 2**20),
        cost_estimate=pl.CostEstimate(flops=int(2e9 * weight), bytes_accessed=int(2**23 * weight), transcendentals=0),
    )(*args)


def start_kernel(
    here, x_hbm, wq_hbm, wk_hbm, wv_hbm, gain_a_hbm, gain_f_hbm, table_hbm, lengths_hbm, *refs
):
    halves, outs, small_ref = refs[:2], refs[2:6], refs[6]
    weights, (gain_a_ref, gain_f_ref, table_ref, lengths_ref), sems = refs[7:10], refs[10:14], refs[14]
    moves = [(x_hbm.at[here[X]], halves[0]), (x_hbm.at[1 - here[X]], halves[1])]
    moves += list(zip((wq_hbm, wk_hbm, wv_hbm), weights))
    moves += [(gain_a_hbm, gain_a_ref), (gain_f_hbm, gain_f_ref), (table_hbm, table_ref), (lengths_hbm, lengths_ref)]
    copies = [pltpu.make_async_copy(src, dst, sems.at[i]) for i, (src, dst) in enumerate(moves)]
    for copy in copies:
        copy.start()
    small_ref[...] = jnp.zeros(small_ref.shape, F32)
    for copy in copies:
        copy.wait()
    small_ref[0:1, :OWN] = gain_a_ref[...].astype(F32).reshape(1, OWN)
    small_ref[1:2, :OWN] = gain_f_ref[...].astype(F32).reshape(1, OWN)
    lengths = lengths_ref[...].reshape(1, SEQ_DEV)
    high = lengths >> 7
    small_ref[2:3, :SEQ_DEV] = high.astype(F32)
    small_ref[3:4, :SEQ_DEV] = (lengths - high * 128).astype(F32)
    small_ref[8:16, :H] = table_ref[...].astype(F32)
    for k in range(TP):

        @pl.when(here[ME] == k)
        def _():
            for r in range(TP):
                for m, ref in enumerate(weights):
                    outs[r][:OWN, m * COLS : (m + 1) * COLS] = ref[:, (k ^ r) * COLS : (k ^ r) * COLS + COLS]

    for out in outs:
        out[OWN:] = small_ref[...].astype(BF16)


def inner_blocks_kernel(here, inner_ref, teacher_ref, near_ref, far_ref, own_ref, core_ref, across_ref):
    near_ref[...] = teacher_ref[here[X]]
    far_ref[...] = teacher_ref[1 - here[X]]

    def lanes(r):
        return pl.ds(pl.multiple_of((here[ME] ^ r) * D, D), D)

    own_ref[...] = inner_ref[:, lanes(0)]
    core_ref[...] = inner_ref[:, lanes(1)]
    rows = across_ref.shape[1]
    for i in range(2):
        across_ref[i] = inner_ref[pl.ds(pl.multiple_of(here[X] * rows, rows), rows), lanes(2 + i)]


def inner_rows_kernel(here, own_ref, core_ref, y_ref, x_ref, core_y_ref, core_x_ref, out_ref):
    rows = y_ref.shape[1]
    me, x = here[ME], here[X]
    out_ref[pl.ds(pl.multiple_of(me * OWN, OWN), OWN)] = own_ref[...]
    out_ref[pl.ds(pl.multiple_of((me ^ 1) * OWN, OWN), OWN)] = core_ref[...]
    for r, ref, half in ((2, y_ref, x), (2, x_ref, 1 - x), (3, core_y_ref, x), (3, core_x_ref, 1 - x)):
        start = (me ^ r) * OWN + half * rows
        out_ref[pl.ds(pl.multiple_of(start, rows), rows)] = ref[r - 2]


def gain_row(small_ref, row):
    return jnp.concatenate([small_ref[i, row : row + 1, :OWN] for i in range(TP)], axis=1)


def bias_kernel(longest, here, small_a, small_b, small_c, small_d, small_ref, info_ref, bias_ref):
    for r, ref in enumerate((small_a, small_b, small_c, small_d)):
        small_ref[here[ME] ^ r] = ref[OWN:].astype(F32)
    pair = lax.broadcasted_iota(jnp.int32, (1, SEQ_DEV), 1)
    length = jnp.zeros((1, 1), F32)
    count = jnp.zeros((1, 1), F32)
    for i in range(TP):
        lengths = small_ref[i, 2:3, :SEQ_DEV] * 128.0 + small_ref[i, 3:4, :SEQ_DEV]
        mine = (pair == here[SEQ_BIT]) & (here[SEQ_OWNER] == i)
        length = length + jnp.sum(jnp.where(mine, lengths, 0.0), axis=1, keepdims=True)
        count = count + jnp.sum(jnp.minimum(lengths, longest), axis=1, keepdims=True)
    info_ref[0:1, :] = jnp.broadcast_to(length, (1, 128))
    info_ref[1:2, :] = jnp.broadcast_to(count, (1, 128))
    table = jnp.concatenate([small_ref[i, 8:16, :] for i in range(TP)], axis=0)
    lane = lax.broadcasted_iota(jnp.int32, table.shape, 1)
    apart = lax.broadcasted_iota(jnp.int32, (PIECE, PIECE), 0) - lax.broadcasted_iota(
        jnp.int32, (PIECE, PIECE), 1
    )
    for head in range(HEADS):
        values = jnp.sum(jnp.where(lane == here[ME] * HEADS + head, table, 0.0), axis=1, keepdims=True)
        for tile in range(5):
            low, high = ((15, 16), (1, 16), (0, 32), (17, 32), (31, 32))[tile]
            ids = bucket_index(apart + (tile - 2) * PIECE)
            total = jnp.broadcast_to(values[low : low + 1], (PIECE, PIECE))
            for b in range(low + 1, high):
                total = jnp.where(ids == b, values[b : b + 1], total)
            bias_ref[head, tile] = total


def block_bias(bias_ref, here, head, key_block, query_block, blocks):
    tiles = []
    for i in range(blocks):
        apart = here[KEY_BLOCKS + key_block] - here[QUERY_BLOCKS + query_block + i]
        tiles.append(bias_ref[head, jnp.clip(apart, -2, 2) + 2])
    return tiles[0] if blocks == 1 else jnp.concatenate(tiles, axis=1)


def attend(chunk, offsets, here, q_ref, kv_ref, info_ref, bias_ref, attn_ref, lse_ref, s_ref, p_ref):
    key_blocks = kv_ref.shape[0] // PIECE
    length = info_ref[0:1, 0:1]
    k_off, v_off = offsets
    blocks = chunk // PIECE
    unroll = key_blocks <= 8
    key_iota = lax.broadcasted_iota(jnp.int32, (PIECE, 1), 0)
    for head in range(HEADS):
        lanes = slice(head * DH, head * DH + DH)
        key_part = kv_ref[:, k_off + head * DH : k_off + head * DH + DH]
        value_part = kv_ref[:, v_off + head * DH : v_off + head * DH + DH]

        def for_queries(q_chunk, carry):
            rows = pl.ds(pl.multiple_of(q_chunk * chunk, chunk), chunk)
            s_ref[...] = dot(key_part, q_ref[rows, lanes], NT)

            def score(index, top):
                at = pl.ds(pl.multiple_of(index * PIECE, PIECE), PIECE)
                tile = s_ref[at, :] + block_bias(bias_ref, here, head, index, q_chunk * blocks, blocks)
                ok = (here[KEY_BLOCKS + index] * PIECE + key_iota).astype(F32) < length
                tile = jnp.where(ok, tile, NEG_FILL)
                s_ref[at, :] = tile
                return jnp.maximum(top, jnp.max(tile, axis=0, keepdims=True))

            top = repeat(key_blocks, unroll, score, jnp.full((1, chunk), NEG_FILL, F32))

            def weigh(index, total):
                at = pl.ds(pl.multiple_of(index * PIECE, PIECE), PIECE)
                weight = jnp.exp(s_ref[at, :] - top)
                p_ref[at, :] = weight.astype(BF16)
                return total + jnp.sum(weight, axis=0, keepdims=True)

            total = repeat(key_blocks, unroll, weigh, jnp.zeros((1, chunk), F32))
            attn_ref[lanes, rows] = dot(value_part, p_ref[...], TN) / total
            lse_ref[head : head + 1, rows] = top + jnp.log(total)
            return carry

        repeat(GROUP // chunk, unroll, for_queries, 0)


def send_kernel(here, partial_ref, send_ref, *_):
    send_ref[...] = partial_ref[2 * ROWS :].astype(BF16)


def stack_rows(here, pieces, out_ref):
    for r, piece in enumerate(pieces):
        out_ref[pl.ds(pl.multiple_of((here[ME] ^ r) * OWN, OWN), OWN)] = piece[:OWN]


def project(here, small_ref, pieces, w_ref, normed_ref, qkv_ref):
    gain = gain_row(small_ref, 0)
    for i, piece in enumerate(pieces):
        values = piece[...].astype(F32)
        normed_ref[i * PIECE : (i + 1) * PIECE] = (values * inverse_rms(values) * gain).astype(BF16)
    qkv_ref[...] = dot(normed_ref[...], w_ref[...]).astype(BF16)


def project_kernel(here, small_ref, *refs):
    project(here, small_ref, refs[:8], *refs[8:])


def attention_kernel(chunk, offsets, here, q_ref, kv_ref, info_ref, bias_ref, out_w_ref, *refs):
    attn_ref, lse_ref, partial_ref, s_ref, p_ref = refs
    attend(chunk, offsets, here, q_ref, kv_ref, info_ref, bias_ref, attn_ref, lse_ref, s_ref, p_ref)
    partial_ref[...] = dot(attn_ref[...].astype(BF16), out_w_ref[...], TN)


def front_kernel(here, small_ref, *refs):
    pieces, (w_ref, info_ref, bias_ref, out_w_ref), (normed_ref, qkv_ref) = refs[:8], refs[8:12], refs[12:14]
    project(here, small_ref, pieces, w_ref, normed_ref, qkv_ref)
    attention_kernel(512, (COLS, 2 * COLS), here, qkv_ref, qkv_ref, info_ref, bias_ref, out_w_ref, *refs[14:])


def attend_back(
    chunk, offsets, here, q_ref, kv_ref, info_ref, bias_ref, out_w_ref, pieces, attn_ref, lse_ref,
    tile_ref, s_ref, dp_ref, p_ref, ds_ref, do_ref, outdot_ref, dqt_ref, dkv_ref,
):
    key_blocks = kv_ref.shape[0] // PIECE
    length = info_ref[0:1, 0:1]
    k_off, v_off = offsets
    blocks = chunk // PIECE
    unroll = key_blocks <= 8
    key_iota = lax.broadcasted_iota(jnp.int32, (PIECE, 1), 0)
    for i, piece in enumerate(pieces):
        at = slice(i * ROWS, (i + 1) * ROWS)
        do_ref[at] = dot(piece[...], out_w_ref[...], NT).astype(BF16)
        do_t = dot(out_w_ref[...], piece[...], NT).astype(BF16).astype(F32) * attn_ref[:, at]
        for head in range(HEADS):
            outdot_ref[head : head + 1, at] = jnp.sum(do_t[head * DH : head * DH + DH], axis=0, keepdims=True)
    tile_ref[...] = jnp.zeros_like(tile_ref)
    dkv_ref[...] = jnp.zeros_like(dkv_ref)
    for head in range(HEADS):
        lanes = slice(head * DH, head * DH + DH)
        v_lanes = slice(COLS + head * DH, COLS + head * DH + DH)
        key_part = kv_ref[:, k_off + head * DH : k_off + head * DH + DH]
        value_part = kv_ref[:, v_off + head * DH : v_off + head * DH + DH]

        def for_queries(q_chunk, carry):
            rows = pl.ds(pl.multiple_of(q_chunk * chunk, chunk), chunk)
            query_part = q_ref[rows, lanes]
            do_part = do_ref[rows, lanes]
            s_ref[...] = dot(key_part, query_part, NT)
            dp_ref[...] = dot(value_part, do_part, NT)
            lse = lse_ref[head : head + 1, rows]
            outdot = outdot_ref[head : head + 1, rows]

            def step(index, carry):
                at = pl.ds(pl.multiple_of(index * PIECE, PIECE), PIECE)
                tile = s_ref[at, :] + block_bias(bias_ref, here, head, index, q_chunk * blocks, blocks)
                ok = (here[KEY_BLOCKS + index] * PIECE + key_iota).astype(F32) < length
                prob = jnp.exp(jnp.where(ok, tile, NEG_FILL) - lse)
                p_ref[at, :] = prob.astype(BF16)
                grad = prob * (dp_ref[at, :] - outdot)
                ds_ref[at, :] = grad.astype(BF16)
                for i in range(blocks):
                    apart = here[KEY_BLOCKS + index] - here[QUERY_BLOCKS + q_chunk * blocks + i]
                    which = jnp.clip(apart, -2, 2) + 2
                    tile_ref[head, which] += grad[:, i * PIECE : (i + 1) * PIECE]
                return carry

            repeat(key_blocks, unroll, step, 0)
            dkv_ref[:, lanes] += dot(ds_ref[...], query_part)
            dkv_ref[:, v_lanes] += dot(p_ref[...], do_part)
            dqt_ref[lanes, rows] = dot(key_part, ds_ref[...], TN)
            return carry

        repeat(GROUP // chunk, unroll, for_queries, 0)


def bucket_sums(tile_ref, head):
    apart = lax.broadcasted_iota(jnp.int32, (PIECE, PIECE), 0) - lax.broadcasted_iota(
        jnp.int32, (PIECE, PIECE), 1
    )
    bucket = lax.broadcasted_iota(jnp.int32, (BUCKETS, 128), 0)
    table = jnp.zeros((BUCKETS, 128), F32)
    for which in range(5):
        tile = tile_ref[head, which]
        low, high = ((15, 16), (1, 16), (0, 32), (17, 32), (31, 32))[which]
        ids = bucket_index(apart + (which - 2) * PIECE)
        for b in range(low, high):
            chosen = tile if high == low + 1 else jnp.where(ids == b, tile, 0.0)
            table = table + jnp.where(bucket == b, jnp.sum(chosen, axis=0, keepdims=True), 0.0)
    return table


def back_scratch(keys, chunk):
    return (
        pltpu.VMEM((keys, chunk), F32),
        pltpu.VMEM((keys, chunk), F32),
        pltpu.VMEM((keys, chunk), BF16),
        pltpu.VMEM((keys, chunk), BF16),
        pltpu.VMEM((GROUP, COLS), BF16),
        pltpu.VMEM((8, GROUP), F32),
        pltpu.VMEM((COLS, GROUP), F32),
        pltpu.VMEM((keys, 2 * COLS), F32),
    )


def join_kernel(here, *refs):
    for i, piece in enumerate(refs[:4]):
        refs[4][i * ROWS : (i + 1) * ROWS] = piece[...]


def attention_back_kernel(chunk, offsets, here, q_ref, kv_ref, info_ref, bias_ref, out_w_ref, attn_ref, lse_ref, *refs):
    pieces, (dq_ref, dkv_low_ref, tile_ref), scratch = refs[:4], refs[4:7], refs[7:]
    attend_back(
        chunk, offsets, here, q_ref, kv_ref, info_ref, bias_ref, out_w_ref, pieces, attn_ref, lse_ref, tile_ref,
        *scratch,
    )
    dq_ref[...] = scratch[6][...].T.astype(BF16)
    dkv_low_ref[...] = scratch[7][...].astype(BF16)


def back_kernel(here, qkv_ref, info_ref, bias_ref, out_w_ref, attn_ref, lse_ref, w_ref, *refs):
    pieces, (d_qkv_ref, tile_ref, partial_ref), scratch = refs[:4], refs[4:7], refs[7:]
    attend_back(
        256, (COLS, 2 * COLS), here, qkv_ref, qkv_ref, info_ref, bias_ref, out_w_ref, pieces, attn_ref, lse_ref,
        tile_ref, *scratch,
    )
    d_qkv_ref[:, :COLS] = scratch[6][...].T.astype(BF16)
    d_qkv_ref[:, COLS:] = scratch[7][...].astype(BF16)
    partial_ref[...] = dot(d_qkv_ref[...], w_ref[...], NT)


def partial_kernel(here, d_ref, w_ref, partial_ref):
    partial_ref[...] = dot(d_ref[...], w_ref[...], NT)


def hidden_kernel(here, small_ref, near_ref, far_ref, keep_ref, core_ref, y_ref, hidden_ref, low_ref):
    rows = jnp.concatenate([near_ref[...], far_ref[...]], axis=0).astype(F32)
    hidden = rows + (keep_ref[:ROWS] + core_ref[:ROWS].astype(F32) + y_ref[...].astype(F32))
    hidden_ref[...] = hidden
    low_ref[...] = (hidden * inverse_rms(hidden) * gain_row(small_ref, 1)).astype(BF16)


def tail_kernel(here, keep_ref, core_ref, out_ref):
    first = 0 if keep_ref.shape[0] == ROWS else ROWS
    kept = keep_ref[first : first + ROWS]
    out_ref[...] = (kept + core_ref[core_ref.shape[0] - ROWS :].astype(F32)).astype(BF16)


def pair_kernel(here, near_ref, far_ref, layer_ref, grad_ref):
    for place, ref in ((here[X], near_ref), (1 - here[X], far_ref)):
        layer_ref[place] = ref[0]
        grad_ref[place] = ref[1].astype(F32)


def sums_kernel(here, partial_ref, normed_ref, small_ref, ffn_gain_ref, squares_ref, tile_ref, out_ref):
    out_ref[...] = jnp.zeros(out_ref.shape, F32)
    products = jnp.sum(partial_ref[...] * normed_ref[...].astype(F32), axis=0, keepdims=True)
    out_ref[0:1] = products / gain_row(small_ref, 0)
    out_ref[1:2] = ffn_gain_ref[...]
    out_ref[2:3] = squares_ref[...]
    lane = lax.broadcasted_iota(jnp.int32, (BUCKETS, 128), 1)
    table = jnp.zeros((BUCKETS, 128), F32)
    for head in range(HEADS):
        values = jnp.sum(bucket_sums(tile_ref, head), axis=1, keepdims=True)
        table = table + jnp.where(lane == here[ME] * HEADS + head, values, 0.0)
    for i in range(TP):
        out_ref[8:16, i * 128 : (i + 1) * 128] = table[i * 8 : (i + 1) * 8]


def small_out(here, info_ref, total, attn_gain_ref, ffn_gain_ref, rows_ref, loss_ref):
    for k in range(TP):

        @pl.when(here[ME] == k)
        def _():
            attn_gain_ref[...] = total[0:1, k * OWN : (k + 1) * OWN]
            ffn_gain_ref[...] = total[1:2, k * OWN : (k + 1) * OWN]
            rows_ref[...] = total[8:16, k * 128 : k * 128 + H]

    loss_ref[...] = jnp.sum(total[2:3], axis=1, keepdims=True) / (info_ref[1:2, 0:1] * D)


def small_out_kernel(here, info_ref, total_ref, *outs):
    small_out(here, info_ref, total_ref[...], *outs)


def rows_kernel(here, a_ref, b_ref, c_ref, d_ref, out_ref):
    stack_rows(here, (a_ref, b_ref, c_ref, d_ref), out_ref)


def ffn_body(values, in_ref, outer_ref, active_ref, slope_ref, keep_ref, send_ref):
    for i, ref in enumerate(values):
        rows = slice(i * ROWS, (i + 1) * ROWS)
        active, slope = gelu_and_slope(dot(ref[...], in_ref[...]))
        active_ref[rows] = active.astype(BF16)
        slope_ref[rows] = slope.astype(BF16)
    partial = dot(active_ref[...], outer_ref[...])
    keep_ref[...] = partial[:ROWS]
    send_ref[...] = partial[ROWS:].astype(BF16)


def ffn_kernel(here, own_ref, core_ref, in_ref, outer_ref, *outs):
    ffn_body((own_ref, core_ref), in_ref, outer_ref, *outs)


def loss_kernel(
    tokens, here, hidden_ref, keep_ref, core_ref, y_ref, near_ref, far_ref, info_ref,
    out_near_ref, out_far_ref, grad_ref, low_ref, square_ref,
):
    length = info_ref[0:1, 0:1]
    factor = tokens / info_ref[1:2, 0:1]
    result = hidden_ref[...] + (keep_ref[...] + core_ref[...].astype(F32) + y_ref[...].astype(F32))
    spot = lax.broadcasted_iota(jnp.int32, (PIECE, 1), 0)
    total = jnp.zeros((1, D), F32)
    for i, (teacher, out) in enumerate(((near_ref, out_near_ref), (far_ref, out_far_ref))):
        rows = slice(i * PIECE, (i + 1) * PIECE)
        part = result[rows]
        out[...] = part.astype(BF16)
        valid = ((here[QUERY_BLOCKS + i] * PIECE + spot).astype(F32) < length).astype(F32)
        deviation = (part - teacher[...].astype(F32)) * valid
        total = total + jnp.sum(deviation * deviation, axis=0, keepdims=True)
        grad = deviation * factor
        grad_ref[rows] = grad
        low_ref[rows] = grad.astype(BF16)
    square_ref[...] = total


def ffn_back_kernel(here, own_ref, core_ref, slope_ref, in_ref, outer_ref, inner_ref, keep_ref, send_ref):
    for i, ref in enumerate((own_ref, core_ref)):
        rows = slice(i * ROWS, (i + 1) * ROWS)
        grad = dot(ref[...], outer_ref[...], NT)
        inner_ref[rows] = (slope_ref[rows].astype(F32) * grad).astype(BF16)
    partial = dot(inner_ref[...], in_ref[...], NT)
    keep_ref[...] = partial[:ROWS]
    send_ref[...] = partial[ROWS:].astype(BF16)


def inner_sum(refs):
    inputs, inner = refs[:4], refs[4:6]
    at = [slice(0, ROWS), slice(ROWS, 2 * ROWS)] * 2
    return sum(dot(inputs[i][...], inner[i // 2][at[i]], TN) for i in range(4))


def outer_half(active_ref, own_ref, core_ref):
    return dot(active_ref[:ROWS], own_ref[...], TN) + dot(active_ref[ROWS:], core_ref[...], TN)


def outer_own_kernel(here, active_ref, own_ref, core_ref, out_ref):
    out_ref[...] = outer_half(active_ref, own_ref, core_ref)


def outer_kernel(here, part_ref, active_ref, own_ref, core_ref, out_ref):
    out_ref[...] = (part_ref[...] + outer_half(active_ref, own_ref, core_ref)).astype(BF16)


def outer_halves_kernel(here, part_ref, active_ref, own_ref, core_ref, send, mine, total_ref):
    total_ref[...] = part_ref[...] + outer_half(active_ref, own_ref, core_ref)
    quarter = D // 8
    for x, out in ((1 - here[X], send), (here[X], mine)):
        for z in range(4):
            start = pl.multiple_of((4 * x + z) * quarter, quarter)
            out[z] = total_ref[pl.ds(start, quarter)].astype(BF16)


def inner_kernel(here, *refs):
    refs[6][...] = inner_sum(refs).astype(BF16)


def inner_halves_kernel(here, *refs):
    send, mine, total_ref = refs[6:]
    total_ref[...] = inner_sum(refs)
    for x, out in ((1 - here[X], send), (here[X], mine)):
        for z in range(4):
            for w in range(TP):
                start = pl.multiple_of(w * OWN + (4 * x + z) * DEPTH, 8)
                out[z * TP + w] = total_ref[pl.ds(start, DEPTH)].astype(BF16)


def hidden_back_kernel(
    here, small_ref, hidden_ref, result_grad_ref, keep_ref, core_ref, y_ref, grad_ref, low_ref, gain_grad_ref
):
    upper = keep_ref[...] + core_ref[...].astype(F32) + y_ref[...].astype(F32)
    back, gain_grad_ref[...] = norm_back(hidden_ref[...], gain_row(small_ref, 1), upper)
    grad = result_grad_ref[...] + back
    grad_ref[...] = grad
    low_ref[...] = grad.astype(BF16)


def qkv_grads(normed_ref, d_qkv_ref, put):
    d_qkv = dot(normed_ref[...], d_qkv_ref[...], TN)
    for m in range(3):
        for i in range(TP):
            block = d_qkv[i * OWN : (i + 1) * OWN, m * COLS : (m + 1) * COLS]
            put(m, slice(i * COLS, (i + 1) * COLS), block)


def attention_grads_kernel(here, normed_ref, d_qkv_ref, attn_ref, up_ref, out_ref):
    def put(m, lanes, block):
        out_ref[m, :, lanes] = block.astype(BF16)

    qkv_grads(normed_ref, d_qkv_ref, put)
    out_ref[3] = dot(attn_ref[...].astype(BF16), up_ref[...]).astype(BF16)


SUM_ROWS = 16


def added(ref, other, index):
    return ref[index].astype(F32) + other[index].astype(F32)


def split_low(here, mine, came, send, keep):
    per = mine.shape[0] // 4
    low = here[Z] & 1
    for high in range(2):
        for i in range(per):
            at = high * per + i
            send[at] = added(mine, came, (2 * high + 1 - low) * per + i).astype(BF16)
            keep[at] = added(mine, came, (2 * high + low) * per + i).astype(BF16)


def split_high(here, mine, came, send, keep, *_):
    per = mine.shape[0] // 2
    high = here[Z] >> 1
    for i in range(per):
        send[i] = added(mine, came, (1 - high) * per + i).astype(BF16)
        keep[i] = added(mine, came, high * per + i).astype(BF16)


def finish(here, mine, came, chunk):
    for i in range(mine.shape[0]):
        chunk[i] = added(mine, came, i).astype(BF16)


def join_high(here, mine, came, pair, per=1):
    high = here[Z] >> 1
    for i in range(per):
        pair[high * per + i] = mine[i]
        pair[(1 - high) * per + i] = came[i]


def join_low(here, mine, came, half, per=1):
    low = here[Z] & 1
    for high in range(2):
        for i in range(per):
            half[(2 * high + low) * per + i] = mine[high * per + i]
            half[(2 * high + 1 - low) * per + i] = came[high * per + i]


def outer_rows(here, half, came, out):
    rows = half.shape[1]
    for x, ref in ((here[X], half), (1 - here[X], came)):
        for z in range(4):
            out[pl.ds(pl.multiple_of((4 * x + z) * rows, 8), rows)] = ref[z].astype(F32)


def send_sums(total, send):
    last = send.shape[0] - 1
    high = total.astype(BF16)
    low = (total - high.astype(F32)).astype(BF16)
    send[last, :8] = high[:8]
    send[last, 8:16] = low[:8]
    send[last, 16:, : TP * 128] = high[8:, : TP * 128]


def sums_of(came):
    last = came.shape[0] - 1
    top = came[last, :8].astype(F32) + came[last, 8:16].astype(F32)
    return jnp.concatenate([top, came[last, 16:].astype(F32)], axis=0)


def out_grads(here, attn_ref, a_ref, b_ref, c_ref, d_ref, send_ref, mine_ref, send, mine, total_ref):
    total = None
    for i, ref in enumerate((a_ref, b_ref, c_ref, d_ref)):
        part = dot(attn_ref[:, i * ROWS : (i + 1) * ROWS].astype(BF16), ref[...])
        total = part if total is None else total + part
    total_ref[...] = total
    for x, ref, out in ((1 - here[X], send_ref, send), (here[X], mine_ref, mine)):
        for z in range(4):
            for w in range(TP):
                out[z * (TP + 1) + w] = ref[z * TP + w]
            start = pl.multiple_of((4 * x + z) * DEPTH, 8)
            out[z * (TP + 1) + TP] = total_ref[pl.ds(start, DEPTH)].astype(BF16)


def inner_finish(here, mine, came, sums, own, *others):
    own[0] = added(mine, came, here[ME]).astype(BF16)
    own[1] = added(mine, came, TP).astype(BF16)
    for r, other in enumerate(others):
        other[0] = added(mine, came, here[ME] ^ (r + 1)).astype(BF16)
        send_sums(sums[...], other)


def inner_collect(here, own, a_ref, b_ref, c_ref, sums, chunk, total):
    for r, ref in enumerate((own, a_ref, b_ref, c_ref)):
        chunk[here[ME] ^ r] = ref[0]
    chunk[TP] = own[1]
    value = sums[...]
    for ref in (a_ref, b_ref, c_ref):
        value = value + sums_of(ref)
    total[...] = value
    send_sums(value, chunk)


def inner_high(here, chunk, came, sums, pair, total):
    join_high(here, chunk, came, pair, TP + 1)
    total[...] = sums[...] + sums_of(came)
    send_sums(total[...], pair)


def inner_low(here, pair, came, sums, half, total):
    join_low(here, pair, came, half, TP + 1)
    total[...] = sums[...] + sums_of(came)
    send_sums(total[...], half)


def inner_rows(here, info_ref, half, came, sums, inner_out, out_out, *small):
    for x, ref in ((here[X], half), (1 - here[X], came)):
        for z in range(4):
            rows = pl.ds(pl.multiple_of((4 * x + z) * DEPTH, 8), DEPTH)
            for w in range(TP):
                inner_out[rows, w * D : (w + 1) * D] = ref[z * (TP + 1) + w].astype(F32)
            out_out[rows] = ref[z * (TP + 1) + TP].astype(F32)
    small_out(here, info_ref, sums[...] + sums_of(came), *small)


def qkv_halves_kernel(here, normed_ref, d_qkv_ref, send, mine, total_ref):
    def put(m, lanes, block):
        total_ref[m, :, lanes] = block

    qkv_grads(normed_ref, d_qkv_ref, put)
    for x, out in ((1 - here[X], send), (here[X], mine)):
        for z in range(4):
            start = pl.multiple_of((4 * x + z) * DEPTH, 8)
            for m in range(3):
                out[z * 3 + m] = total_ref[m, pl.ds(start, DEPTH), :].astype(BF16)


def qkv_finish(here, mine, came, *outs):
    for k in range(TP):

        @pl.when(here[ME] == k)
        def _():
            for m in range(3):
                values = added(mine, came, m).astype(BF16)
                for r, out in enumerate(outs):
                    out[m] = values[:, (k ^ r) * COLS : (k ^ r) * COLS + COLS]


def qkv_collect(here, own, a_ref, b_ref, c_ref, chunk):
    for k in range(TP):

        @pl.when(here[ME] == k)
        def _():
            for m in range(3):
                for r, ref in enumerate((own, a_ref, b_ref, c_ref)):
                    chunk[m, :, (k ^ r) * COLS : (k ^ r) * COLS + COLS] = ref[m]


def qkv_high(here, chunk, came, pair):
    join_high(here, chunk, came, pair, 3)


def qkv_low(here, pair, came, half):
    join_low(here, pair, came, half, 3)


def qkv_rows(here, half, came, *outs):
    for x, ref in ((here[X], half), (1 - here[X], came)):
        for z in range(4):
            for m, out in enumerate(outs):
                out[pl.ds(pl.multiple_of((4 * x + z) * DEPTH, 8), DEPTH)] = ref[z * 3 + m].astype(F32)


def input_kernel(
    here, small_ref, near_ref, far_ref, hidden_grad_ref, keep_ref, core_ref, layer_near_ref, layer_far_ref, y_ref,
    out_near_ref, out_far_ref,
):
    values = jnp.concatenate([near_ref[...], far_ref[...]], axis=0).astype(F32)
    upper = keep_ref[:ROWS] + core_ref[:ROWS].astype(F32) + y_ref[...].astype(F32)
    back, _ = norm_back(values, gain_row(small_ref, 0), upper)
    grad = (hidden_grad_ref[...] + back).astype(BF16)
    out_near_ref[0] = layer_near_ref[...]
    out_near_ref[1] = grad[:PIECE]
    out_far_ref[0] = layer_far_ref[...]
    out_far_ref[1] = grad[PIECE:]


def on_device(
    inputs, teacher, seq_lengths, gain_attn, w_query, w_key, w_value, w_out, bias_table, gain_ffn, w_inner, w_outer
):
    n_ctx = lax.axis_size("ctx")
    spread = n_ctx // (SEQ_DEV * TP)
    me = lax.axis_index("wsh")
    ctx_me = lax.axis_index("ctx")
    parity = ctx_me & 1
    token_total = ROWS * n_ctx * TP
    same, cross = seq_routes(n_ctx)
    home = ctx_me // spread
    stretch = ctx_me % spread
    seq_bit = home & 1
    by_steps = n_ctx == 8

    def to_home(pair):
        return lax.ppermute(pair[0], AXES, same), lax.ppermute(pair[1], AXES, cross)

    def from_home(near, far):
        near = lax.ppermute(near, AXES, backwards(same))
        far = lax.ppermute(far, AXES, backwards(cross))
        return near, far

    def block_places(stretch_index):
        return [
            TP * 2 * stretch_index + 2 * swapped(me ^ r) + (seq_bit ^ e) for r in ORDER for e in (0, 1)
        ]

    query_blocks = block_places(stretch)
    key_blocks = [p for i in range(spread) for p in block_places(i)] if spread > 1 else query_blocks

    scalars = [me, parity, (ctx_me >> 1) & 3, swapped(home >> 1), seq_bit] + query_blocks + key_blocks
    here = jnp.stack([jnp.asarray(v, jnp.int32) for v in scalars])

    low = functools.partial(shape, dtype=BF16)
    x_here, x_there, *qkv_blocks = call(
        start_kernel,
        (low(PIECE, D),) * 2 + (low(OWN + 16, 3 * COLS),) * 4,
        (here, inputs, w_query, w_key, w_value, gain_attn, gain_ffn, bias_table, seq_lengths),
        scratch=(pltpu.VMEM((16, 3 * COLS), F32),) + (pltpu.VMEM((OWN, D), BF16),) * 3
        + (pltpu.VMEM((OWN,), BF16),) * 2 + (pltpu.VMEM((8, H), BF16), pltpu.VMEM((SEQ_DEV,), jnp.int32))
        + (pltpu.SemaphoreType.DMA((9,)),),
        mib=START_MIB,
        in_hbm=8,
    )
    x_near, x_far = to_home((x_here, x_there))

    def group_blocks(values):
        return (values[0],) + tuple(to_partner(values[r], r) for r in (1, 2, 3))

    w_qkv_pieces = group_blocks(qkv_blocks)
    (small, info, bias), (w_qkv,) = run(
        here,
        (
            functools.partial(bias_kernel, float(n_ctx * PIECE)),
            (shape(TP, 16, 3 * COLS), shape(8, 128), shape(HEADS, 5, PIECE, PIECE)),
            w_qkv_pieces,
        ),
        (rows_kernel, (low(D, 3 * COLS),), w_qkv_pieces),
    )
    x_own = (x_near, x_far)
    *teacher_halves, in_own, in_core, in_across = call(
        inner_blocks_kernel,
        (low(PIECE, D),) * 2 + (low(OWN, D),) * 2 + (low(2, OWN // 2, D),),
        (here, after(w_inner, w_qkv), teacher),
    )
    x_y = tuple(to_partner(v, 2) for v in x_own)
    x_y = tuple(after(v, w_qkv) for v in x_y)
    pieces = x_own + x_y + tuple(to_partner(v, 1) for v in x_own + x_y)
    attn_shapes = (shape(COLS, GROUP), shape(8, GROUP), shape(GROUP, D))
    send_job = (send_kernel, (low(2 * ROWS, D),))
    proj_shapes = (low(GROUP, D), low(GROUP, 3 * COLS))

    def attn_scratch(keys, chunk):
        return (pltpu.VMEM((keys, chunk), F32), pltpu.VMEM((keys, chunk), BF16))

    if spread == 1:
        normed, qkv, attn_t, lse, partial = call(
            front_kernel,
            proj_shapes + attn_shapes,
            (here, small) + pieces + (w_qkv, info, bias, w_out),
            scratch=attn_scratch(GROUP, 512),
            mib=14,
        )
    else:
        teams = [[s * spread + i for i in range(spread)] for s in range(SEQ_DEV * TP)]
        normed, qkv = call(project_kernel, proj_shapes, (here, small) + pieces + (w_qkv,))
        kv = lax.all_gather(qkv[:, COLS:], "ctx", axis=0, tiled=True, axis_index_groups=teams)
        q = qkv[:, :COLS]
        attn_t, lse, partial = call(
            functools.partial(attention_kernel, 128, (0, COLS)),
            attn_shapes,
            (here, q, kv, info, bias, w_out),
            scratch=attn_scratch(kv.shape[0], 128),
            mib=56,
        )

    def scatter_tail(keep_y, from_core):
        return call(tail_kernel, (low(ROWS, D),), (here, keep_y, from_core))[0]

    from_y = to_partner(after(in_across, *x_y), 2)
    teacher_near, teacher_far = to_home([after(v, *x_y) for v in teacher_halves])
    partial, from_y, teacher_near, teacher_far = lax.optimization_barrier((partial, from_y, teacher_near, teacher_far))
    ((send,),) = run(here, send_job + ((partial,),))
    core = to_partner(send, 1)
    from_x = to_ctx(after(from_y, send), 1)
    in_core = to_partner(after(in_core, send), 1)
    going = scatter_tail(partial, core)
    across = to_partner(going, 2)
    hidden, ffn_low = call(
        hidden_kernel,
        (shape(ROWS, D), low(ROWS, D)),
        (here, small, x_near, x_far, partial, core, across),
    )
    core_y, core_x = to_partner(after(from_y, send), 1), to_partner(after(from_x, ffn_low), 1)
    (w_in,) = call(
        inner_rows_kernel, (low(D, D),), (here, after(in_own, ffn_low), in_core, from_y, from_x, core_y, core_x)
    )

    def gathered(value):
        from_y = to_partner(value, 2)
        return to_partner(value, 1), from_y

    def both_halves(first_call, second_call, value):
        from_core, from_y = gathered(value)
        first, done = first_call((value, from_core))
        core_y = to_partner(after(from_y, done), 1)
        second = second_call((from_y, core_y))
        core_own = to_partner(first[-1], 1)
        going = scatter_tail(second[-2], to_partner(second[-1], 1))
        across = to_partner(going, 2)
        return (value, from_core, from_y, core_y), first, second, (first[-2], core_own, across), going

    half = low(2 * ROWS, D)
    piece_shapes = (shape(ROWS, D), low(ROWS, D))
    def ffn(values):
        return call(ffn_kernel, (half, half) + piece_shapes, (here,) + values + (w_in, w_outer))

    def ffn_first(values):
        outs = ffn(values)
        return outs, outs[-1]

    ffn_all, (active_a, slope_a, *_), (active_b, slope_b, *_), parts, _ = both_halves(ffn_first, ffn, ffn_low)
    out_near, out_far, result_grad, result_low, squares = call(
        functools.partial(loss_kernel, float(token_total)),
        (low(PIECE, D), low(PIECE, D), shape(ROWS, D), low(ROWS, D), shape(1, D)),
        (here, hidden) + parts + (teacher_near, teacher_far, info),
    )

    depth = OWN // n_ctx

    def parts_of(count, rows=DEPTH):
        return low(count, rows, D)

    def ffn_back(values, slope):
        return call(ffn_back_kernel, (half,) + piece_shapes, (here,) + values + (slope, w_in, w_outer))

    def ffn_back_first(values):
        outs = ffn_back(values, slope_a)
        (part,) = call(
            outer_own_kernel, (shape(D, D),), (here, after(active_a, outs[-1])) + values, mib=12
        )
        grads.append(part)
        return outs, part

    def ffn_back_second(values):
        args = (here, grads[0], active_b) + values
        if by_steps:
            outs = (parts_of(4, D // 8),) * 2
            grads[:] = call(outer_halves_kernel, outs, args, scratch=(pltpu.VMEM((D, D), F32),), mib=14)
        else:
            grads[:] = call(outer_kernel, (low(D, D),), args, mib=12)
        return ffn_back((after(values[0], grads[0]), values[1]), slope_b)

    grads = []
    result_all, (inner_a, *_), (inner_b, *_), parts, going = both_halves(
        ffn_back_first, ffn_back_second, result_low
    )
    inner_args = (here,) + ffn_all + (inner_a, after(inner_b, going))
    ahead = []
    if by_steps:
        outer_send, outer_mine = grads
        outer_came = to_ctx(outer_send, 1)
        inner_send, inner_mine = call(
            inner_halves_kernel, (parts_of(4 * TP),) * 2, inner_args, scratch=(pltpu.VMEM((D, D), F32),), mib=14
        )
        ordered = inner_send
        ahead.append((split_low, (parts_of(2, D // 8),) * 2, (outer_mine, outer_came)))
    else:
        (outer_wgrad,) = grads
        (inner_wgrad,) = call(inner_kernel, (low(D, D),), inner_args, mib=14)
        ordered = inner_wgrad
    (hidden_grad, hidden_low, ffn_gain_grad), *ahead = run(
        here,
        (
            hidden_back_kernel,
            (shape(ROWS, D), low(ROWS, D), shape(1, D)),
            (small, after(hidden, ordered), result_grad) + parts,
        ),
        *ahead,
    )
    from_core, from_y = gathered(hidden_low)
    if by_steps:
        ((outer_send, outer_keep),) = ahead
        outer_came = to_ctx(outer_send, 2)
        from_y = after(from_y, outer_came)
    up_pieces = (hidden_low, from_y, from_core, to_partner(from_y, 1))
    table_shape = shape(HEADS, 5, PIECE, PIECE)
    if by_steps:
        (inner_send, inner_mine), (outer_send, outer_keep) = run(
            here,
            (
                out_grads,
                (parts_of(4 * TP + 4),) * 2,
                (attn_t,) + up_pieces + (inner_send, inner_mine),
            ),
            (split_high, (parts_of(1, D // 8),) * 2, (outer_keep, outer_came)),
            scratch=(pltpu.VMEM((OWN, D), F32),),
        )
        inner_came = to_ctx(inner_send, 1)
        outer_came = to_ctx(outer_send, 4)
        up_pieces = (after(hidden_low, outer_keep),) + up_pieces[1:]
    if spread == 1:
        d_qkv, table_part, partial = call(
            back_kernel,
            (proj_shapes[1], table_shape, shape(GROUP, D)),
            (here, qkv, info, bias, w_out, attn_t, lse, w_qkv) + up_pieces,
            scratch=back_scratch(GROUP, 256),
            mib=20,
        )
    else:
        dq, dkv, table_part = call(
            functools.partial(attention_back_kernel, 128, (0, COLS)),
            (low(GROUP, COLS), low(kv.shape[0], 2 * COLS), table_shape),
            (here, q, kv, info, bias, w_out, attn_t, lse) + up_pieces,
            scratch=back_scratch(kv.shape[0], 128),
            mib=60,
        )
        dkv = lax.psum_scatter(dkv, "ctx", scatter_dimension=0, tiled=True, axis_index_groups=teams)
        d_qkv = jnp.concatenate([dq, dkv], axis=1)
        (partial,) = call(partial_kernel, (shape(GROUP, D),), (here, d_qkv, w_qkv))
    if by_steps:
        (send,), (outer_chunk,), (inner_send, inner_keep) = run(
            here,
            send_job + ((partial,),),
            (finish, (parts_of(1, D // 8),), (outer_keep, outer_came)),
            (split_low, (parts_of(2 * TP + 2),) * 2, (inner_mine, inner_came)),
        )
        outer_came = to_ctx(outer_chunk, 4)
        inner_came = to_ctx(inner_send, 2)
    else:
        ((send,),) = run(here, send_job + ((partial,),))
    core = to_partner(send, 1)
    input_job = (
        input_kernel,
        (low(2, PIECE, D), low(2, PIECE, D)),
        (small, x_near, x_far, hidden_grad, partial, core, out_near, out_far),
    )
    small_shapes = (shape(1, OWN), shape(1, OWN), shape(8, H), shape(1, 1))
    sums_shape = shape(SUM_ROWS, D)
    pair_out = (low(SEQ_DEV, PIECE, D), shape(SEQ_DEV, PIECE, D))
    sum_args = (partial, normed, small, ffn_gain_grad, squares, table_part)

    if by_steps:
        going = scatter_tail(partial, core)
        across = to_partner(going, 2)
        qkv_send, qkv_mine = call(
            qkv_halves_kernel,
            (parts_of(12),) * 2,
            (here, normed, after(d_qkv, going)),
            scratch=(pltpu.VMEM((3, OWN, D), F32),),
        )
        qkv_came = to_ctx(qkv_send, 1)
        inner_keep, across = lax.optimization_barrier((after(inner_keep, qkv_send), across))
        (inner_send, inner_keep), (outer_pair,) = run(
            here,
            (split_high, (parts_of(TP + 1),) * 2, (inner_keep, inner_came)),
            (join_high, (parts_of(2, D // 8),), (outer_chunk, outer_came)),
        )
        inner_came = to_ctx(inner_send, 4)
        outer_came = to_ctx(outer_pair, 2)
        ((in_near, in_far),) = run(
            here, (input_job[0], input_job[1], input_job[2] + (after(across, inner_keep),))
        )
        home_near, home_far = from_home(in_near, in_far)
        ((qkv_send, qkv_keep),) = run(
            here, (split_low, (parts_of(6),) * 2, (after(qkv_mine, in_near), qkv_came))
        )
        qkv_came = to_ctx(qkv_send, 2)
        (sums,) = call(sums_kernel, (sums_shape,), (here, after(partial, qkv_send)) + sum_args[1:])
        inner_blocks, (outer_half,) = run(
            here,
            (
                inner_finish,
                (parts_of(2),) + (parts_of(1 + 1),) * 3,
                (after(inner_keep, qkv_keep), inner_came, sums),
            ),
            (join_low, (parts_of(4, D // 8),), (outer_pair, outer_came)),
        )
        inner_blocks = group_blocks(inner_blocks)
        outer_came = to_ctx(outer_half, 1)
        ((qkv_send, qkv_keep),) = run(
            here, (split_high, (parts_of(3),) * 2, (after(qkv_keep, outer_half), qkv_came))
        )
        qkv_came = to_ctx(qkv_send, 4)
        ((inner_chunk, sums),) = run(
            here,
            (
                inner_collect,
                (parts_of(TP + 1 + 1), sums_shape),
                (after(inner_blocks[0], qkv_keep, home_far),) + inner_blocks[1:] + (sums,),
            ),
        )
        inner_came = to_ctx(inner_chunk, 4)
        (qkv_blocks,) = run(
            here, (qkv_finish, (low(3, DEPTH, COLS),) * 4, (after(qkv_keep, inner_chunk), qkv_came))
        )
        qkv_blocks = group_blocks(qkv_blocks)
        (inner_pair, sums), (w_outer_grad,) = run(
            here,
            (
                inner_high,
                (parts_of(2 * TP + 2 + 1), sums_shape),
                (after(inner_chunk, qkv_blocks[0]), inner_came, sums),
            ),
            (outer_rows, (shape(D, D),), (outer_half, outer_came)),
        )
        inner_came = to_ctx(inner_pair, 2)
        ((qkv_chunk,),) = run(
            here, (qkv_collect, (parts_of(3),), (after(qkv_blocks[0], inner_pair),) + qkv_blocks[1:])
        )
        qkv_came = to_ctx(qkv_chunk, 4)
        ((inner_half, sums),) = run(
            here,
            (
                inner_low,
                (parts_of(4 * TP + 4 + 1), sums_shape),
                (after(inner_pair, qkv_chunk), inner_came, sums),
            ),
        )
        inner_came = to_ctx(inner_half, 1)
        ((qkv_pair,),) = run(here, (qkv_high, (parts_of(6),), (after(qkv_chunk, inner_half), qkv_came)))
        qkv_came = to_ctx(qkv_pair, 2)
        ((qkv_half,),) = run(here, (qkv_low, (parts_of(12),), (qkv_pair, qkv_came)))
        qkv_came = to_ctx(qkv_half, 1)
        ((w_inner_grad, w_out_grad, my_attn_gain, my_ffn_gain, my_rows, loss_value),) = run(
            here,
            (
                inner_rows,
                (shape(OWN, TP * D), shape(OWN, D)) + small_shapes,
                (info, after(inner_half, qkv_half), inner_came, sums),
            ),
        )
        (layer_out, input_grad), (w_query_grad, w_key_grad, w_value_grad) = run(
            here,
            (pair_kernel, pair_out, (home_near, home_far)),
            (qkv_rows, (shape(OWN, D),) * 3, (after(qkv_half, w_out_grad), qkv_came)),
        )
    else:
        across = to_partner(scatter_tail(partial, core), 2)
        ((in_near, in_far),) = run(here, (input_job[0], input_job[1], input_job[2] + (across,)))
        ((layer_out, input_grad),) = run(here, (pair_kernel, pair_out, from_home(in_near, in_far)))
        (sums,) = call(sums_kernel, (sums_shape,), (here,) + sum_args)
        (hidden_all,) = call(join_kernel, (low(GROUP, D),), (here,) + up_pieces)
        my_attn_gain, my_ffn_gain, my_rows, loss_value = call(
            small_out_kernel, small_shapes, (here, info, lax.psum(sums, AXES))
        )

        def summed(parts):
            return lax.psum_scatter(parts, "ctx", scatter_dimension=0)

        def inner_to_rows(chunk):
            return swap_blocks(chunk, "wsh").transpose(1, 0, 2).reshape(depth, TP * D)

        def attn_to_rows(chunk):
            blocks = chunk[:3].reshape(3, depth, TP, COLS).transpose(2, 0, 1, 3)
            mine = swap_blocks(blocks, "wsh").transpose(1, 2, 0, 3).reshape(3, depth, D)
            return jnp.concatenate([mine, chunk[3:]])

        (attn_wgrad,) = call(
            attention_grads_kernel, (low(4, OWN, D),), (here, normed, d_qkv, attn_t, hidden_all)
        )
        outer_full = lax.all_gather(summed(outer_wgrad.reshape(n_ctx, D // n_ctx, D)), "ctx")
        inner_parts = inner_wgrad.reshape(TP, n_ctx, depth, D).transpose(1, 0, 2, 3)
        inner_full = lax.all_gather(inner_to_rows(summed(inner_parts)), "ctx")
        attn_parts = attn_wgrad.reshape(4, n_ctx, depth, D).transpose(1, 0, 2, 3)
        attn_full = lax.all_gather(attn_to_rows(summed(attn_parts)), "ctx")
        w_outer_grad = outer_full.reshape(D, D).astype(F32)
        w_inner_grad = inner_full.reshape(OWN, TP * D).astype(F32)
        w_query_grad, w_key_grad, w_value_grad, w_out_grad = (
            attn_full[:, m].reshape(OWN, D).astype(F32) for m in range(4)
        )

    return (
        layer_out,
        loss_value.reshape(()),
        input_grad,
        my_attn_gain.reshape(-1),
        w_query_grad,
        w_key_grad,
        w_value_grad,
        w_out_grad,
        my_rows,
        my_ffn_gain.reshape(-1),
        w_inner_grad,
        w_outer_grad,
    )


def solution(mesh):
    rows = P("wsh", None)
    tokens = P("wsh", "ctx", None)
    return jax.shard_map(
        on_device,
        mesh=mesh,
        in_specs=(tokens, tokens, P("wsh"), P("wsh"), rows, rows, rows, rows, rows, P("wsh"), rows, rows),
        out_specs=(tokens, P(), tokens, P("wsh"), rows, rows, rows, rows, rows, P("wsh"), rows, rows),
        check_vma=False,
    )
```

profile of v0, /device:TPU:4, one launch (start us, length us, event | category | flops | bytes accessed | tf_op | source)
XLA Modules:
  0.0 282.2 jit_solution(10078511292035215126)
XLA Ops:
  1.4 3.5 %start_kernel.1 = (bf16[128,768]{1,0:T(8,128)(2,1)}, bf16[128,768]{1,0:T(8,128)(2,1)}, bf16[208,576]{1,0:T(8,128)(2,1)}, bf16[208,576]{1,0:T(8,128)(2,1)}, bf16[...) custom-call(s32[21]{0:T(128)} %stack.60.here, bf16[2,128,768]{2,1,0:T(8,128)(2,1)} %x_hbm.1, bf16[192,768]{1,0:T(8,128)(2,1)} %wq_hbm.1, ...), custom_call_target="tpu_custom_call" | custom-call | flops 2000000000 | bytes 8388608 | tf_op jit(solution)/shard_map/start_kernel/pallas_call | solution.py:157
  6.8 2.5 collective-permute-start.4
  9.3 3.3 %collective-permute-start.3 = (bf16[128,768]{1,0:T(8,128)(2,1)}, bf16[128,768]{1,0:T(8,128)(2,1)S(1)}, u32[]{:S(2)}, u32[]{:S(2)}) collective-permute-start(bf16[128,768]{1,0:T(8,128)(2,1)} %get-tuple-element.155), channel_id=1, source_target_pairs={{0,0},{1,16},{2,8},{3,24},{4,4},{5,20},{6,12},{7,28},{8,2},{9,18},... | collective-permute-start | bytes 589832 | tf_op jit(solution)/shard_map/ppermute | solution.py:823
  12.6 9.8 %collective-permute-done.4.refs_1_.far_ref.refs_2_ = bf16[128,768]{1,0:T(8,128)(2,1)S(1)} collective-permute-done((bf16[128,768]{1,0:T(8,128)(2,1)}, bf16[128,768]{1,0:T(8,128)(2,1)S(1)}, u32[]{:S(2)}, u32[]{:S(2)}) %collective-permute-start.4) | collective-permute-done | bytes 196640 | tf_op jit(solution)/shard_map/ppermute | solution.py:823
  22.4 2.6 collective-permute-done.3.refs_0_.near_ref.refs_1_
  30.2 2.6 collective-permute-done.6.refs_3_
  32.8 3.8 %collective-permute-done.5.refs_2_ = bf16[128,768]{1,0:T(8,128)(2,1)S(1)} collective-permute-done((bf16[128,768]{1,0:T(8,128)(2,1)S(1)}, bf16[128,768]{1,0:T(8,128)(2,1)S(1)}, u32[]{:S(2)}, u32[]{:S(2)}) %collective-permute-start.5) | collective-permute-done | bytes 196640 | tf_op jit(solution)/shard_map/ppermute | solution.py:66
  37.8 2.5 collective-permute-start.13
  40.3 3.5 %collective-permute-start.12 = (bf16[128,768]{1,0:T(8,128)(2,1)S(1)}, bf16[128,768]{1,0:T(8,128)(2,1)S(1)}, u32[]{:S(2)}, u32[]{:S(2)}) collective-permute-start(bf16[128,768]{1,0:T(8,128)(2,1)S(1)} %get-tuple-element.167), channel_id=1, source_target_pairs={{0,0},{1,16},{2,8},{3,24},{4,4},{5,20},{6,12},{7,28},{8,2},{9,18},... | collective-permute-start | bytes 589832 | tf_op jit(solution)/shard_map/ppermute | solution.py:823
  43.8 8.8 %front_kernel.1 = (bf16[1024,768]{1,0:T(8,128)(2,1)S(1)}, bf16[1024,576]{1,0:T(8,128)(2,1)S(1)}, f32[192,1024]{1,0:T(8,128)S(1)}, f32[8,1024]{1,0:T(8,128)S(1)}, f32[1024,768]{1,0:T(8,128)S(1)}) custom-call(s32[21]{0:T(128)S(1)} %copy-done, f32[4,16,576]{2,1,0:T(8,128)S(1)} %get-tuple-element.154.small_ref.refs_0_, ...), custom_call_target="tpu_custom_call" | custom-call | flops 2000000000 | bytes 8388608 | tf_op jit(solution)/shard_map/front_kernel/pallas_call | solution.py:157
  61.5 9.2 %collective-permute-done.15.y_ref = bf16[256,768]{1,0:T(8,128)(2,1)S(1)} collective-permute-done((bf16[256,768]{1,0:T(8,128)(2,1)S(1)}, bf16[256,768]{1,0:T(8,128)(2,1)S(1)}, u32[]{:S(2)}, u32[]{:S(2)}) %collective-permute-start.15) | collective-permute-done | bytes 393248 | tf_op jit(solution)/shard_map/ppermute | solution.py:66
  76.0 7.3 %collective-permute-done.17.own_ref.refs_2_ = bf16[256,768]{1,0:T(8,128)(2,1)S(1)} collective-permute-done((bf16[256,768]{1,0:T(8,128)(2,1)S(1)}, bf16[256,768]{1,0:T(8,128)(2,1)S(1)}, u32[]{:S(2)}, u32[]{:S(2)}) %collective-permute-start.17) | collective-permute-done | bytes 393248 | tf_op jit(solution)/shard_map/ppermute | solution.py:66
  89.9 10.9 %collective-permute-done.25.y_ref = bf16[256,768]{1,0:T(8,128)(2,1)S(1)} collective-permute-done((bf16[256,768]{1,0:T(8,128)(2,1)S(1)}, bf16[256,768]{1,0:T(8,128)(2,1)S(1)}, u32[]{:S(2)}, u32[]{:S(2)}) %collective-permute-start.25) | collective-permute-done | bytes 393248 | tf_op jit(solution)/shard_map/ppermute | solution.py:66
  107.2 6.5 %collective-permute-done.27.own_ref = bf16[256,768]{1,0:T(8,128)(2,1)S(1)} collective-permute-done((bf16[256,768]{1,0:T(8,128)(2,1)S(1)}, bf16[256,768]{1,0:T(8,128)(2,1)S(1)}, u32[]{:S(2)}, u32[]{:S(2)}) %collective-permute-start.27) | collective-permute-done | bytes 393248 | tf_op jit(solution)/shard_map/ppermute | solution.py:66
  123.8 10.9 %collective-permute-done.32.refs_7_ = bf16[4,96,768]{2,1,0:T(8,128)(2,1)S(1)} collective-permute-done((bf16[4,96,768]{2,1,0:T(8,128)(2,1)S(1)}, bf16[4,96,768]{2,1,0:T(8,128)(2,1)S(1)}, u32[]{:S(2)}, u32[]{:S(2)}) %collective-permute-start.32) | collective-permute-done | bytes 589856 | tf_op jit(solution)/shard_map/ppermute | solution.py:71
  137.3 7.3 %collective-permute-done.34.refs_8_ = bf16[2,96,768]{2,1,0:T(8,128)(2,1)S(1)} collective-permute-done((bf16[2,96,768]{2,1,0:T(8,128)(2,1)S(1)}, bf16[2,96,768]{2,1,0:T(8,128)(2,1)S(1)}, u32[]{:S(2)}, u32[]{:S(2)}) %collective-permute-start.34) | collective-permute-done | bytes 294944 | tf_op jit(solution)/shard_map/ppermute | solution.py:71
  152.8 13.4 %back_kernel.1 = (bf16[1024,576]{1,0:T(8,128)(2,1)S(1)}, f32[3,5,128,128]{3,2,1,0:T(8,128)S(1)}, f32[1024,768]{1,0:T(8,128)S(1)}) custom-call(s32[21]{0:T(128)S(1)} %copy-done, bf16[1024,576]{1,0:T(8,128)(2,1)S(1)} %get-tuple-element.208.qkv_ref, f32[8,128]{1,0:T(8,128)S(1)} %get-tuple-element.160.refs_9_.info_ref.refs_0_, ...), custom_call_target="tpu_custom_call" | custom-call | flops 2000000000 | bytes 8388608 | tf_op jit(solution)/shard_map/back_kernel/pallas_call | solution.py:157
  173.2 2.6 collective-permute-start.42
  179.5 3.6 %collective-permute-done.40.refs_8_ = bf16[256,768]{1,0:T(8,128)(2,1)S(1)} collective-permute-done((bf16[256,768]{1,0:T(8,128)(2,1)S(1)}, bf16[256,768]{1,0:T(8,128)(2,1)S(1)}, u32[]{:S(2)}, u32[]{:S(2)}) %collective-permute-start.40) | collective-permute-done | bytes 393248 | tf_op jit(solution)/shard_map/ppermute | solution.py:66
  193.7 2.8 sums_kernel.1.refs_2_.refs_4_
  198.2 3.8 %collective-permute-done.47.refs_4_ = bf16[2,96,768]{2,1,0:T(8,128)(2,1)S(1)} collective-permute-done((bf16[2,96,768]{2,1,0:T(8,128)(2,1)S(1)}, bf16[2,96,768]{2,1,0:T(8,128)(2,1)S(1)}, u32[]{:S(2)}, u32[]{:S(2)}) %collective-permute-start.47) | collective-permute-done | bytes 294944 | tf_op jit(solution)/shard_map/ppermute | solution.py:71
  204.0 7.0 %collective-permute-start.50 = (bf16[2,24,768]{2,1,0:T(8,128)(2,1)S(1)}, bf16[2,24,768]{2,1,0:T(8,128)(2,1)S(1)}, u32[]{:S(2)}, u32[]{:S(2)}) collective-permute-start(bf16[2,24,768]{2,1,0:T(8,128)(2,1)S(1)} %get-tuple-element.256), channel_id=1, source_target_pairs={{0,2},{1,3},{2,0},{3,1},{4,6},{5,7},{6,4},{7,5},{8,10},{9,11},{10,... | collective-permute-start | bytes 221192 | tf_op jit(solution)/shard_map/ppermute | solution.py:66
  214.6 2.9 %collective-permute-done.44.refs_1_ = bf16[2,128,768]{2,1,0:T(8,128)(2,1)S(1)} collective-permute-done((bf16[2,128,768]{2,1,0:T(8,128)(2,1)S(1)}, bf16[2,128,768]{2,1,0:T(8,128)(2,1)S(1)}, u32[]{:S(2)}, u32[]{:S(2)}) %collective-permute-start.44) | collective-permute-done | bytes 393248 | tf_op jit(solution)/shard_map/ppermute | solution.py:827
  221.0 3.4 %collective-permute-done.52.refs_1_ = bf16[3,24,768]{2,1,0:T(8,128)(2,1)S(1)} collective-permute-done((bf16[3,24,768]{2,1,0:T(8,128)(2,1)S(1)}, bf16[3,24,768]{2,1,0:T(8,128)(2,1)S(1)}, u32[]{:S(2)}, u32[]{:S(2)}) %collective-permute-start.52) | collective-permute-done | bytes 110624 | tf_op jit(solution)/shard_map/ppermute | solution.py:71
  225.1 8.8 %collective-permute-done.53.refs_1_ = bf16[6,24,768]{2,1,0:T(8,128)(2,1)S(1)} collective-permute-done((bf16[6,24,768]{2,1,0:T(8,128)(2,1)S(1)}, bf16[6,24,768]{2,1,0:T(8,128)(2,1)S(1)}, u32[]{:S(2)}, u32[]{:S(2)}) %collective-permute-start.53) | collective-permute-done | bytes 221216 | tf_op jit(solution)/shard_map/ppermute | solution.py:71
  238.3 2.9 %collective-permute-done.56.refs_2_ = bf16[3,24,192]{2,1,0:T(8,128)(2,1)S(1)} collective-permute-done((bf16[3,24,192]{2,1,0:T(8,128)(2,1)S(1)}, bf16[3,24,192]{2,1,0:T(8,128)(2,1)S(1)}, u32[]{:S(2)}, u32[]{:S(2)}) %collective-permute-start.56) | collective-permute-done | bytes 27680 | tf_op jit(solution)/shard_map/ppermute | solution.py:66
  241.8 3.0 %collective-permute-start.59 = (bf16[3,24,768]{2,1,0:T(8,128)(2,1)S(1)}, bf16[3,24,768]{2,1,0:T(8,128)(2,1)S(1)}, u32[]{:S(2)}, u32[]{:S(2)}) collective-permute-start(bf16[3,24,768]{2,1,0:T(8,128)(2,1)S(1)} %qkv_collect.1.refs_0_), channel_id=1, source_target_pairs={{0,16},{4,20},{8,24},{12,28},{16,0},{20,4},{24,8},{28,12},{1,17},{... | collective-permute-start | bytes 331784 | tf_op jit(solution)/shard_map/ppermute | solution.py:71
  244.8 5.5 %collective-permute-done.58.refs_1_ = bf16[11,24,768]{2,1,0:T(8,128)(2,1)S(1)} collective-permute-done((bf16[11,24,768]{2,1,0:T(8,128)(2,1)S(1)}, bf16[11,24,768]{2,1,0:T(8,128)(2,1)S(1)}, u32[]{:S(2)}, u32[]{:S(2)}) %collective-permute-start.58) | collective-permute-done | bytes 405536 | tf_op jit(solution)/shard_map/ppermute | solution.py:71
  253.1 6.9 %collective-permute-done.60.refs_1_ = bf16[6,24,768]{2,1,0:T(8,128)(2,1)S(1)} collective-permute-done((bf16[6,24,768]{2,1,0:T(8,128)(2,1)S(1)}, bf16[6,24,768]{2,1,0:T(8,128)(2,1)S(1)}, u32[]{:S(2)}, u32[]{:S(2)}) %collective-permute-start.60) | collective-permute-done | bytes 221216 | tf_op jit(solution)/shard_map/ppermute | solution.py:71
  263.3 7.9 %collective-permute-done.61.refs_2_ = bf16[21,24,768]{2,1,0:T(8,128)(2,1)S(1)} collective-permute-done((bf16[21,24,768]{2,1,0:T(8,128)(2,1)S(1)}, bf16[21,24,768]{2,1,0:T(8,128)(2,1)S(1)}, u32[]{:S(2)}, u32[]{:S(2)}) %collective-permute-start.61) | collective-permute-done | bytes 774176 | tf_op jit(solution)/shard_map/ppermute | solution.py:71
  271.2 2.4 inner_rows.1
  273.5 4.6 %collective-permute-done.43.refs_0_ = bf16[2,128,768]{2,1,0:T(8,128)(2,1)S(1)} collective-permute-done((bf16[2,128,768]{2,1,0:T(8,128)(2,1)S(1)}, bf16[2,128,768]{2,1,0:T(8,128)(2,1)S(1)}, u32[]{:S(2)}, u32[]{:S(2)}) %collective-permute-start.43) | collective-permute-done | bytes 393248 | tf_op jit(solution)/shard_map/ppermute | solution.py:826
  (146 shorter events, 104.6 us)
Async XLA Ops:
  4.9 20.2 %collective-permute-start = (bf16[208,576]{1,0:T(8,128)(2,1)}, bf16[208,576]{1,0:T(8,128)(2,1)S(1)}, u32[]{:S(2)}, u32[]{:S(2)}) collective-permute-start(bf16[208,576]{1,0:T(8,128)(2,1)} %get-tuple-element.151), channel_id=1, source_target_pairs={{0,1},{1,0},{2,3},{3,2},{4,5},{5,4},{6,7},{7,6},{8,9},{9,8},{10,11... | collective-permute-start | bytes 718856 | tf_op jit(solution)/shard_map/ppermute | solution.py:66
  4.9 20.1 %collective-permute-start.1 = (bf16[208,576]{1,0:T(8,128)(2,1)}, bf16[208,576]{1,0:T(8,128)(2,1)S(1)}, u32[]{:S(2)}, u32[]{:S(2)}) collective-permute-start(bf16[208,576]{1,0:T(8,128)(2,1)} %get-tuple-element.152), channel_id=1, source_target_pairs={{0,2},{1,3},{2,0},{3,1},{4,6},{5,7},{6,4},{7,5},{8,10},{9,11},{10,... | collective-permute-start | bytes 718856 | tf_op jit(solution)/shard_map/ppermute | solution.py:66
  5.0 22.6 %collective-permute-start.2 = (bf16[208,576]{1,0:T(8,128)(2,1)}, bf16[208,576]{1,0:T(8,128)(2,1)S(1)}, u32[]{:S(2)}, u32[]{:S(2)}) collective-permute-start(bf16[208,576]{1,0:T(8,128)(2,1)} %get-tuple-element.153), channel_id=1, source_target_pairs={{0,3},{1,2},{2,1},{3,0},{4,7},{5,6},{6,5},{7,4},{8,11},{9,10},{10,... | collective-permute-start | bytes 718856 | tf_op jit(solution)/shard_map/ppermute | solution.py:66
  6.8 15.6 %collective-permute-start.4 = (bf16[128,768]{1,0:T(8,128)(2,1)}, bf16[128,768]{1,0:T(8,128)(2,1)S(1)}, u32[]{:S(2)}, u32[]{:S(2)}) collective-permute-start(bf16[128,768]{1,0:T(8,128)(2,1)} %get-tuple-element.156), channel_id=1, source_target_pairs={{0,4},{1,20},{2,12},{3,28},{4,0},{5,16},{6,8},{7,24},{8,6},{9,22},... | collective-permute-start | bytes 589832 | tf_op jit(solution)/shard_map/ppermute | solution.py:823
  9.3 15.8 %collective-permute-start.3 = (bf16[128,768]{1,0:T(8,128)(2,1)}, bf16[128,768]{1,0:T(8,128)(2,1)S(1)}, u32[]{:S(2)}, u32[]{:S(2)}) collective-permute-start(bf16[128,768]{1,0:T(8,128)(2,1)} %get-tuple-element.155), channel_id=1, source_target_pairs={{0,0},{1,16},{2,8},{3,24},{4,4},{5,20},{6,12},{7,28},{8,2},{9,18},... | collective-permute-start | bytes 589832 | tf_op jit(solution)/shard_map/ppermute | solution.py:823
  25.0 11.5 %collective-permute-start.5 = (bf16[128,768]{1,0:T(8,128)(2,1)S(1)}, bf16[128,768]{1,0:T(8,128)(2,1)S(1)}, u32[]{:S(2)}, u32[]{:S(2)}) collective-permute-start(bf16[128,768]{1,0:T(8,128)(2,1)S(1)} %collective-permute-done.3.refs_0_.near_ref.refs_1_), channel_id=1, source_target_pairs={{0,2},{1,3},{2,0},{3,1},{4,6},{5,7},{6,4},{7,5},{8,10},{9,11},{10,... | collective-permute-start | bytes 589832 | tf_op jit(solution)/shard_map/ppermute | solution.py:66
  25.0 12.7 %collective-permute-start.7 = (bf16[128,768]{1,0:T(8,128)(2,1)S(1)}, bf16[128,768]{1,0:T(8,128)(2,1)S(1)}, u32[]{:S(2)}, u32[]{:S(2)}) collective-permute-start(bf16[128,768]{1,0:T(8,128)(2,1)S(1)} %collective-permute-done.3.refs_0_.near_ref.refs_1_), channel_id=1, source_target_pairs={{0,1},{1,0},{2,3},{3,2},{4,5},{5,4},{6,7},{7,6},{8,9},{9,8},{10,11... | collective-permute-start | bytes 589832 | tf_op jit(solution)/shard_map/ppermute | solution.py:66
  25.1 15.2 %collective-permute-start.8 = (bf16[128,768]{1,0:T(8,128)(2,1)S(1)}, bf16[128,768]{1,0:T(8,128)(2,1)S(1)}, u32[]{:S(2)}, u32[]{:S(2)}) collective-permute-start(bf16[128,768]{1,0:T(8,128)(2,1)S(1)} %collective-permute-done.4.refs_1_.far_ref.refs_2_), channel_id=1, source_target_pairs={{0,1},{1,0},{2,3},{3,2},{4,5},{5,4},{6,7},{7,6},{8,9},{9,8},{10,11... | collective-permute-start | bytes 589832 | tf_op jit(solution)/shard_map/ppermute | solution.py:66
  37.7 18.2 %collective-permute-start.11 = (bf16[2,96,768]{2,1,0:T(8,128)(2,1)S(1)}, bf16[2,96,768]{2,1,0:T(8,128)(2,1)S(1)}, u32[]{:S(2)}, u32[]{:S(2)}) collective-permute-start(bf16[2,96,768]{2,1,0:T(8,128)(2,1)S(1)} %get-tuple-element.165), channel_id=1, source_target_pairs={{0,2},{1,3},{2,0},{3,1},{4,6},{5,7},{6,4},{7,5},{8,10},{9,11},{10,... | collective-permute-start | bytes 884744 | tf_op jit(solution)/shard_map/ppermute | solution.py:66
  37.8 16.0 %collective-permute-start.13 = (bf16[128,768]{1,0:T(8,128)(2,1)S(1)}, bf16[128,768]{1,0:T(8,128)(2,1)S(1)}, u32[]{:S(2)}, u32[]{:S(2)}) collective-permute-start(bf16[128,768]{1,0:T(8,128)(2,1)S(1)} %get-tuple-element.169), channel_id=1, source_target_pairs={{0,4},{1,20},{2,12},{3,28},{4,0},{5,16},{6,8},{7,24},{8,6},{9,22},... | collective-permute-start | bytes 589832 | tf_op jit(solution)/shard_map/ppermute | solution.py:823
  40.3 15.6 %collective-permute-start.12 = (bf16[128,768]{1,0:T(8,128)(2,1)S(1)}, bf16[128,768]{1,0:T(8,128)(2,1)S(1)}, u32[]{:S(2)}, u32[]{:S(2)}) collective-permute-start(bf16[128,768]{1,0:T(8,128)(2,1)S(1)} %get-tuple-element.167), channel_id=1, source_target_pairs={{0,0},{1,16},{2,8},{3,24},{4,4},{5,20},{6,12},{7,28},{8,2},{9,18},... | collective-permute-start | bytes 589832 | tf_op jit(solution)/shard_map/ppermute | solution.py:823
  59.6 12.0 %collective-permute-start.19 = (bf16[2,96,768]{2,1,0:T(8,128)(2,1)S(1)}, bf16[2,96,768]{2,1,0:T(8,128)(2,1)S(1)}, u32[]{:S(2)}, u32[]{:S(2)}) collective-permute-start(bf16[2,96,768]{2,1,0:T(8,128)(2,1)S(1)} %collective-permute-done.11.y_ref), channel_id=1, source_target_pairs={{0,4},{4,0},{8,12},{12,8},{16,20},{20,16},{24,28},{28,24},{1,5},{5... | collective-permute-start | bytes 884744 | tf_op jit(solution)/shard_map/ppermute | solution.py:71
  61.0 11.5 %collective-permute-start.20 = (bf16[2,96,768]{2,1,0:T(8,128)(2,1)S(1)}, bf16[2,96,768]{2,1,0:T(8,128)(2,1)S(1)}, u32[]{:S(2)}, u32[]{:S(2)}) collective-permute-start(bf16[2,96,768]{2,1,0:T(8,128)(2,1)S(1)} %collective-permute-done.11.y_ref), channel_id=1, source_target_pairs={{0,1},{1,0},{2,3},{3,2},{4,5},{5,4},{6,7},{7,6},{8,9},{9,8},{10,11... | collective-permute-start | bytes 884744 | tf_op jit(solution)/shard_map/ppermute | solution.py:66
  61.0 11.5 %collective-permute-start.18 = (bf16[192,768]{1,0:T(8,128)(2,1)S(1)}, bf16[192,768]{1,0:T(8,128)(2,1)S(1)}, u32[]{:S(2)}, u32[]{:S(2)}) collective-permute-start(bf16[192,768]{1,0:T(8,128)(2,1)S(1)} %get-tuple-element.176), channel_id=1, source_target_pairs={{0,1},{1,0},{2,3},{3,2},{4,5},{5,4},{6,7},{7,6},{8,9},{9,8},{10,11... | collective-permute-start | bytes 884744 | tf_op jit(solution)/shard_map/ppermute | solution.py:66
  102.1 11.5 %collective-permute-start.27 = (bf16[256,768]{1,0:T(8,128)(2,1)S(1)}, bf16[256,768]{1,0:T(8,128)(2,1)S(1)}, u32[]{:S(2)}, u32[]{:S(2)}) collective-permute-start(bf16[256,768]{1,0:T(8,128)(2,1)S(1)} %get-tuple-element.187.own_ref), channel_id=1, source_target_pairs={{0,2},{1,3},{2,0},{3,1},{4,6},{5,7},{6,4},{7,5},{8,10},{9,11},{10,... | collective-permute-start | bytes 1179656 | tf_op jit(solution)/shard_map/ppermute | solution.py:66
  119.1 15.6 %collective-permute-start.32 = (bf16[4,96,768]{2,1,0:T(8,128)(2,1)S(1)}, bf16[4,96,768]{2,1,0:T(8,128)(2,1)S(1)}, u32[]{:S(2)}, u32[]{:S(2)}) collective-permute-start(bf16[4,96,768]{2,1,0:T(8,128)(2,1)S(1)} %get-tuple-element.195), channel_id=1, source_target_pairs={{0,4},{4,0},{8,12},{12,8},{16,20},{20,16},{24,28},{28,24},{1,5},{5... | collective-permute-start | bytes 1769480 | tf_op jit(solution)/shard_map/ppermute | solution.py:71
  121.3 13.4 %collective-permute-start.31 = (bf16[256,768]{1,0:T(8,128)(2,1)S(1)}, bf16[256,768]{1,0:T(8,128)(2,1)S(1)}, u32[]{:S(2)}, u32[]{:S(2)}) collective-permute-start(bf16[256,768]{1,0:T(8,128)(2,1)S(1)} %tail_kernel.6), channel_id=1, source_target_pairs={{0,2},{1,3},{2,0},{3,1},{4,6},{5,7},{6,4},{7,5},{8,10},{9,11},{10,... | collective-permute-start | bytes 1179656 | tf_op jit(solution)/shard_map/ppermute | solution.py:66
  149.5 18.6 %collective-permute-start.38 = (bf16[20,24,768]{2,1,0:T(8,128)(2,1)S(1)}, bf16[20,24,768]{2,1,0:T(8,128)(2,1)S(1)}, u32[]{:S(2)}, u32[]{:S(2)}) collective-permute-start(bf16[20,24,768]{2,1,0:T(8,128)(2,1)S(1)} %get-tuple-element.221), channel_id=1, source_target_pairs={{0,4},{4,0},{8,12},{12,8},{16,20},{20,16},{24,28},{28,24},{1,5},{5... | collective-permute-start | bytes 2211848 | tf_op jit(solution)/shard_map/ppermute | solution.py:71
  150.9 15.3 %collective-permute-start.37 = (bf16[1,96,768]{2,1,0:T(8,128)(2,1)S(1)}, bf16[1,96,768]{2,1,0:T(8,128)(2,1)S(1)}, u32[]{:S(2)}, u32[]{:S(2)}) collective-permute-start(bf16[1,96,768]{2,1,0:T(8,128)(2,1)S(1)} %get-tuple-element.219), channel_id=1, source_target_pairs={{0,16},{4,20},{8,24},{12,28},{16,0},{20,4},{24,8},{28,12},{1,17},{... | collective-permute-start | bytes 442376 | tf_op jit(solution)/shard_map/ppermute | solution.py:71
  172.3 13.6 %collective-permute-start.41 = (bf16[10,24,768]{2,1,0:T(8,128)(2,1)S(1)}, bf16[10,24,768]{2,1,0:T(8,128)(2,1)S(1)}, u32[]{:S(2)}, u32[]{:S(2)}) collective-permute-start(bf16[10,24,768]{2,1,0:T(8,128)(2,1)S(1)} %get-tuple-element.233), channel_id=1, source_target_pairs={{0,8},{4,12},{8,0},{12,4},{16,24},{20,28},{24,16},{28,20},{1,9},{5... | collective-permute-start | bytes 1105928 | tf_op jit(solution)/shard_map/ppermute | solution.py:71
  177.9 14.7 %collective-permute-start.45 = (bf16[12,24,768]{2,1,0:T(8,128)(2,1)S(1)}, bf16[12,24,768]{2,1,0:T(8,128)(2,1)S(1)}, u32[]{:S(2)}, u32[]{:S(2)}) collective-permute-start(bf16[12,24,768]{2,1,0:T(8,128)(2,1)S(1)} %get-tuple-element.229), channel_id=1, source_target_pairs={{0,4},{4,0},{8,12},{12,8},{16,20},{20,16},{24,28},{28,24},{1,5},{5... | collective-permute-start | bytes 1327112 | tf_op jit(solution)/shard_map/ppermute | solution.py:71
  189.4 12.6 %collective-permute-start.47 = (bf16[2,96,768]{2,1,0:T(8,128)(2,1)S(1)}, bf16[2,96,768]{2,1,0:T(8,128)(2,1)S(1)}, u32[]{:S(2)}, u32[]{:S(2)}) collective-permute-start(bf16[2,96,768]{2,1,0:T(8,128)(2,1)S(1)} %get-tuple-element.249.refs_3_), channel_id=1, source_target_pairs={{0,8},{4,12},{8,0},{12,4},{16,24},{20,28},{24,16},{28,20},{1,9},{5... | collective-permute-start | bytes 884744 | tf_op jit(solution)/shard_map/ppermute | solution.py:71
  191.1 26.4 %collective-permute-start.44 = (bf16[2,128,768]{2,1,0:T(8,128)(2,1)S(1)}, bf16[2,128,768]{2,1,0:T(8,128)(2,1)S(1)}, u32[]{:S(2)}, u32[]{:S(2)}) collective-permute-start(bf16[2,128,768]{2,1,0:T(8,128)(2,1)S(1)} %get-tuple-element.238), channel_id=1, source_target_pairs={{4,0},{20,1},{12,2},{28,3},{0,4},{16,5},{8,6},{24,7},{6,8},{22,9},... | collective-permute-start | bytes 1179656 | tf_op jit(solution)/shard_map/ppermute | solution.py:827
  193.3 18.8 %collective-permute-start.48 = (bf16[6,24,768]{2,1,0:T(8,128)(2,1)S(1)}, bf16[6,24,768]{2,1,0:T(8,128)(2,1)S(1)}, u32[]{:S(2)}, u32[]{:S(2)}) collective-permute-start(bf16[6,24,768]{2,1,0:T(8,128)(2,1)S(1)} %get-tuple-element.244), channel_id=1, source_target_pairs={{0,8},{4,12},{8,0},{12,4},{16,24},{20,28},{24,16},{28,20},{1,9},{5... | collective-permute-start | bytes 663560 | tf_op jit(solution)/shard_map/ppermute | solution.py:71
  202.6 31.3 %collective-permute-start.54 = (bf16[4,96,768]{2,1,0:T(8,128)(2,1)S(1)}, bf16[4,96,768]{2,1,0:T(8,128)(2,1)S(1)}, u32[]{:S(2)}, u32[]{:S(2)}) collective-permute-start(bf16[4,96,768]{2,1,0:T(8,128)(2,1)S(1)} %get-tuple-element.250.refs_3_), channel_id=1, source_target_pairs={{0,4},{4,0},{8,12},{12,8},{16,20},{20,16},{24,28},{28,24},{1,5},{5... | collective-permute-start | bytes 1769480 | tf_op jit(solution)/shard_map/ppermute | solution.py:71
  204.0 13.5 %collective-permute-start.49 = (bf16[2,24,768]{2,1,0:T(8,128)(2,1)S(1)}, bf16[2,24,768]{2,1,0:T(8,128)(2,1)S(1)}, u32[]{:S(2)}, u32[]{:S(2)}) collective-permute-start(bf16[2,24,768]{2,1,0:T(8,128)(2,1)S(1)} %get-tuple-element.255), channel_id=1, source_target_pairs={{0,1},{1,0},{2,3},{3,2},{4,5},{5,4},{6,7},{7,6},{8,9},{9,8},{10,11... | collective-permute-start | bytes 221192 | tf_op jit(solution)/shard_map/ppermute | solution.py:66
  204.0 14.2 %collective-permute-start.50 = (bf16[2,24,768]{2,1,0:T(8,128)(2,1)S(1)}, bf16[2,24,768]{2,1,0:T(8,128)(2,1)S(1)}, u32[]{:S(2)}, u32[]{:S(2)}) collective-permute-start(bf16[2,24,768]{2,1,0:T(8,128)(2,1)S(1)} %get-tuple-element.256), channel_id=1, source_target_pairs={{0,2},{1,3},{2,0},{3,1},{4,6},{5,7},{6,4},{7,5},{8,10},{9,11},{10,... | collective-permute-start | bytes 221192 | tf_op jit(solution)/shard_map/ppermute | solution.py:66
  219.6 14.3 %collective-permute-start.53 = (bf16[6,24,768]{2,1,0:T(8,128)(2,1)S(1)}, bf16[6,24,768]{2,1,0:T(8,128)(2,1)S(1)}, u32[]{:S(2)}, u32[]{:S(2)}) collective-permute-start(bf16[6,24,768]{2,1,0:T(8,128)(2,1)S(1)} %get-tuple-element.262.refs_0_), channel_id=1, source_target_pairs={{0,16},{4,20},{8,24},{12,28},{16,0},{20,4},{24,8},{28,12},{1,17},{... | collective-permute-start | bytes 663560 | tf_op jit(solution)/shard_map/ppermute | solution.py:71
  236.0 14.3 %collective-permute-start.58 = (bf16[11,24,768]{2,1,0:T(8,128)(2,1)S(1)}, bf16[11,24,768]{2,1,0:T(8,128)(2,1)S(1)}, u32[]{:S(2)}, u32[]{:S(2)}) collective-permute-start(bf16[11,24,768]{2,1,0:T(8,128)(2,1)S(1)} %get-tuple-element.269.refs_0_), channel_id=1, source_target_pairs={{0,8},{4,12},{8,0},{12,4},{16,24},{20,28},{24,16},{28,20},{1,9},{5... | collective-permute-start | bytes 1216520 | tf_op jit(solution)/shard_map/ppermute | solution.py:71
  251.0 20.2 %collective-permute-start.61 = (bf16[21,24,768]{2,1,0:T(8,128)(2,1)S(1)}, bf16[21,24,768]{2,1,0:T(8,128)(2,1)S(1)}, u32[]{:S(2)}, u32[]{:S(2)}) collective-permute-start(bf16[21,24,768]{2,1,0:T(8,128)(2,1)S(1)} %get-tuple-element.273.refs_1_), channel_id=1, source_target_pairs={{0,4},{4,0},{8,12},{12,8},{16,20},{20,16},{24,28},{28,24},{1,5},{5... | collective-permute-start | bytes 2322440 | tf_op jit(solution)/shard_map/ppermute | solution.py:71
  260.5 19.2 %collective-permute-start.62 = (bf16[12,24,768]{2,1,0:T(8,128)(2,1)S(1)}, bf16[12,24,768]{2,1,0:T(8,128)(2,1)S(1)}, u32[]{:S(2)}, u32[]{:S(2)}) collective-permute-start(bf16[12,24,768]{2,1,0:T(8,128)(2,1)S(1)} %qkv_low.1.refs_2_), channel_id=1, source_target_pairs={{0,4},{4,0},{8,12},{12,8},{16,20},{20,16},{24,28},{28,24},{1,5},{5... | collective-permute-start | bytes 1327112 | tf_op jit(solution)/shard_map/ppermute | solution.py:71
  261.4 16.7 %collective-permute-start.43 = (bf16[2,128,768]{2,1,0:T(8,128)(2,1)S(1)}, bf16[2,128,768]{2,1,0:T(8,128)(2,1)S(1)}, u32[]{:S(2)}, u32[]{:S(2)}) collective-permute-start(bf16[2,128,768]{2,1,0:T(8,128)(2,1)S(1)} %get-tuple-element.237), channel_id=1, source_target_pairs={{0,0},{16,1},{8,2},{24,3},{4,4},{20,5},{12,6},{28,7},{2,8},{18,9},... | collective-permute-start | bytes 1179656 | tf_op jit(solution)/shard_map/ppermute | solution.py:826
  (37 other events, 245.2 us)
where the time goes:
time: 285 us; the launch traced here: 282 us
  waiting for transfers between devices  152 us (53%)
  Pallas kernels  69 us (24%)
  starting transfers between devices  57.8 us (20%)
    pallas_call x39, Pallas kernels, call(): pl.pallas_call(body, name=name_of(body), out_shape=tuple(outs), in_specs=...  69 us
    ppermute x38, waiting for transfers between devices, to_partner(): return lax.ppermute(value, 'wsh', [(i, i ^ offset) for i in range(TP)])  65.6 us
    ppermute x19, waiting for transfers between devices, to_ctx(): return lax.ppermute(value, 'ctx', [(i, i ^ offset) for i in range(n_ctx)])  63.6 us
    ppermute x19, starting transfers between devices, to_ctx(): return lax.ppermute(value, 'ctx', [(i, i ^ offset) for i in range(n_ctx)])  24.3 us
    ppermute x38, starting transfers between devices, to_partner(): return lax.ppermute(value, 'wsh', [(i, i ^ offset) for i in range(TP)])  18.3 us
    ppermute x2, waiting for transfers between devices, to_home(): lax.ppermute(pair[1], AXES, cross)  11 us
    ppermute x2, starting transfers between devices, to_home(): lax.ppermute(pair[0], AXES, same)  6.77 us
  transfers between devices with their start and end apart: 63, of which 41 were waited for; matrix products, arithmetic and copies ran while one was open for 0% of the time, Pallas kernels for 17%

commit v1 on v0

--- a/solution.py
+++ b/solution.py
@@ -996,18 +996,18 @@
         (outer_wgrad,) = grads
         (inner_wgrad,) = call(inner_kernel, (low(D, D),), inner_args, mib=14)
         ordered = inner_wgrad
-    (hidden_grad, hidden_low, ffn_gain_grad), *ahead = run(
+    ((hidden_grad, hidden_low, ffn_gain_grad),) = run(
         here,
         (
             hidden_back_kernel,
             (shape(ROWS, D), low(ROWS, D), shape(1, D)),
             (small, after(hidden, ordered), result_grad) + parts,
         ),
-        *ahead,
     )
     from_core, from_y = gathered(hidden_low)
     if by_steps:
-        ((outer_send, outer_keep),) = ahead
+        body, outs, args = ahead[0]
+        ((outer_send, outer_keep),) = run(here, (body, outs, (after(args[0], hidden_low),) + args[1:]))
         outer_came = to_ctx(outer_send, 2)
         from_y = after(from_y, outer_came)
     up_pieces = (hidden_low, from_y, from_core, to_partner(from_y, 1))

time: 285 us -> 283 us (level)
    ppermute x19, waiting for transfers between devices: 63.6 us -> 54.9 us  [to_ctx(): return lax.ppermute(value, 'ctx', [(i, i ^ offset) for i in range(n_ctx)])]
    ppermute x38, waiting for transfers between devices: 65.6 us -> 71.8 us  [to_partner(): return lax.ppermute(value, 'wsh', [(i, i ^ offset) for i in range(TP)])]
    pallas_call x39 -> x40, Pallas kernels: 69 us -> 69.5 us  [call(): pl.pallas_call(body, name=name_of(body), out_shape=tuple(outs), in_specs=...]
  transfers between devices with their start and end apart: 63 -> 63, of which waited for: 41 -> 40; matrix products, arithmetic and copies ran while one was open for 0% -> 0% of each run, Pallas kernels for 17% -> 18%
where the time goes in v1:
time: 283 us; the launch traced here: 280 us
  waiting for transfers between devices  150 us (53%)
  Pallas kernels  69.5 us (25%)
  starting transfers between devices  56.8 us (20%)
    ppermute x38, waiting for transfers between devices, to_partner(): return lax.ppermute(value, 'wsh', [(i, i ^ offset) for i in range(TP)])  71.8 us
    pallas_call x40, Pallas kernels, call(): pl.pallas_call(body, name=name_of(body), out_shape=tuple(outs), in_specs=...  69.5 us
    ppermute x19, waiting for transfers between devices, to_ctx(): return lax.ppermute(value, 'ctx', [(i, i ^ offset) for i in range(n_ctx)])  54.9 us
    ppermute x19, starting transfers between devices, to_ctx(): return lax.ppermute(value, 'ctx', [(i, i ^ offset) for i in range(n_ctx)])  23.5 us
    ppermute x38, starting transfers between devices, to_partner(): return lax.ppermute(value, 'wsh', [(i, i ^ offset) for i in range(TP)])  18 us
    ppermute x2, waiting for transfers between devices, to_home(): lax.ppermute(pair[1], AXES, cross)  11 us
    ppermute x2, starting transfers between devices, to_home(): lax.ppermute(pair[0], AXES, same)  6.77 us
  transfers between devices with their start and end apart: 63, of which 40 were waited for; matrix products, arithmetic and copies ran while one was open for 0% of the time, Pallas kernels for 18%

profile of v1, /device:TPU:4, one launch (start us, length us, event | category | flops | bytes accessed | tf_op | source)
XLA Modules:
  0.0 279.5 jit_solution(14081277968521296211)
XLA Ops:
  1.3 3.5 %start_kernel.1 = (bf16[128,768]{1,0:T(8,128)(2,1)}, bf16[128,768]{1,0:T(8,128)(2,1)}, bf16[208,576]{1,0:T(8,128)(2,1)}, bf16[208,576]{1,0:T(8,128)(2,1)}, bf16[...) custom-call(s32[21]{0:T(128)} %stack.60.here, bf16[2,128,768]{2,1,0:T(8,128)(2,1)} %x_hbm.1, bf16[192,768]{1,0:T(8,128)(2,1)} %wq_hbm.1, ...), custom_call_target="tpu_custom_call" | custom-call | flops 2000000000 | bytes 8388608 | tf_op jit(solution)/shard_map/start_kernel/pallas_call | solution.py:157
  6.8 2.5 collective-permute-start.4
  9.2 3.3 %collective-permute-start.3 = (bf16[128,768]{1,0:T(8,128)(2,1)}, bf16[128,768]{1,0:T(8,128)(2,1)S(1)}, u32[]{:S(2)}, u32[]{:S(2)}) collective-permute-start(bf16[128,768]{1,0:T(8,128)(2,1)} %get-tuple-element.156), channel_id=1, source_target_pairs={{0,0},{1,16},{2,8},{3,24},{4,4},{5,20},{6,12},{7,28},{8,2},{9,18},... | collective-permute-start | bytes 589832 | tf_op jit(solution)/shard_map/ppermute | solution.py:823
  12.5 9.8 %collective-permute-done.4.refs_1_.far_ref.refs_2_ = bf16[128,768]{1,0:T(8,128)(2,1)S(1)} collective-permute-done((bf16[128,768]{1,0:T(8,128)(2,1)}, bf16[128,768]{1,0:T(8,128)(2,1)S(1)}, u32[]{:S(2)}, u32[]{:S(2)}) %collective-permute-start.4) | collective-permute-done | bytes 196640 | tf_op jit(solution)/shard_map/ppermute | solution.py:823
  22.3 2.6 collective-permute-done.3.refs_0_.near_ref.refs_1_
  30.1 2.6 collective-permute-done.6.refs_3_
  32.7 3.8 %collective-permute-done.5.refs_2_ = bf16[128,768]{1,0:T(8,128)(2,1)S(1)} collective-permute-done((bf16[128,768]{1,0:T(8,128)(2,1)S(1)}, bf16[128,768]{1,0:T(8,128)(2,1)S(1)}, u32[]{:S(2)}, u32[]{:S(2)}) %collective-permute-start.5) | collective-permute-done | bytes 196640 | tf_op jit(solution)/shard_map/ppermute | solution.py:66
  37.7 2.5 collective-permute-start.13
  40.2 3.5 %collective-permute-start.12 = (bf16[128,768]{1,0:T(8,128)(2,1)S(1)}, bf16[128,768]{1,0:T(8,128)(2,1)S(1)}, u32[]{:S(2)}, u32[]{:S(2)}) collective-permute-start(bf16[128,768]{1,0:T(8,128)(2,1)S(1)} %get-tuple-element.168), channel_id=1, source_target_pairs={{0,0},{1,16},{2,8},{3,24},{4,4},{5,20},{6,12},{7,28},{8,2},{9,18},... | collective-permute-start | bytes 589832 | tf_op jit(solution)/shard_map/ppermute | solution.py:823
  43.7 8.8 %front_kernel.1 = (bf16[1024,768]{1,0:T(8,128)(2,1)S(1)}, bf16[1024,576]{1,0:T(8,128)(2,1)S(1)}, f32[192,1024]{1,0:T(8,128)S(1)}, f32[8,1024]{1,0:T(8,128)S(1)}, f32[1024,768]{1,0:T(8,128)S(1)}) custom-call(s32[21]{0:T(128)S(1)} %copy-done, f32[4,16,576]{2,1,0:T(8,128)S(1)} %get-tuple-element.155.small_ref.refs_0_, ...), custom_call_target="tpu_custom_call" | custom-call | flops 2000000000 | bytes 8388608 | tf_op jit(solution)/shard_map/front_kernel/pallas_call | solution.py:157
  61.4 9.2 %collective-permute-done.15.y_ref = bf16[256,768]{1,0:T(8,128)(2,1)S(1)} collective-permute-done((bf16[256,768]{1,0:T(8,128)(2,1)S(1)}, bf16[256,768]{1,0:T(8,128)(2,1)S(1)}, u32[]{:S(2)}, u32[]{:S(2)}) %collective-permute-start.15) | collective-permute-done | bytes 393248 | tf_op jit(solution)/shard_map/ppermute | solution.py:66
  75.9 7.3 %collective-permute-done.17.own_ref.refs_2_ = bf16[256,768]{1,0:T(8,128)(2,1)S(1)} collective-permute-done((bf16[256,768]{1,0:T(8,128)(2,1)S(1)}, bf16[256,768]{1,0:T(8,128)(2,1)S(1)}, u32[]{:S(2)}, u32[]{:S(2)}) %collective-permute-start.17) | collective-permute-done | bytes 393248 | tf_op jit(solution)/shard_map/ppermute | solution.py:66
  89.8 10.9 %collective-permute-done.25.y_ref = bf16[256,768]{1,0:T(8,128)(2,1)S(1)} collective-permute-done((bf16[256,768]{1,0:T(8,128)(2,1)S(1)}, bf16[256,768]{1,0:T(8,128)(2,1)S(1)}, u32[]{:S(2)}, u32[]{:S(2)}) %collective-permute-start.25) | collective-permute-done | bytes 393248 | tf_op jit(solution)/shard_map/ppermute | solution.py:66
  107.1 6.5 %collective-permute-done.27.own_ref = bf16[256,768]{1,0:T(8,128)(2,1)S(1)} collective-permute-done((bf16[256,768]{1,0:T(8,128)(2,1)S(1)}, bf16[256,768]{1,0:T(8,128)(2,1)S(1)}, u32[]{:S(2)}, u32[]{:S(2)}) %collective-permute-start.27) | collective-permute-done | bytes 393248 | tf_op jit(solution)/shard_map/ppermute | solution.py:66
  123.8 8.6 %collective-permute-done.31.refs_5_ = bf16[256,768]{1,0:T(8,128)(2,1)S(1)} collective-permute-done((bf16[256,768]{1,0:T(8,128)(2,1)S(1)}, bf16[256,768]{1,0:T(8,128)(2,1)S(1)}, u32[]{:S(2)}, u32[]{:S(2)}) %collective-permute-start.31) | collective-permute-done | bytes 393248 | tf_op jit(solution)/shard_map/ppermute | solution.py:66
  135.6 8.1 %collective-permute-done.34.refs_8_ = bf16[2,96,768]{2,1,0:T(8,128)(2,1)S(1)} collective-permute-done((bf16[2,96,768]{2,1,0:T(8,128)(2,1)S(1)}, bf16[2,96,768]{2,1,0:T(8,128)(2,1)S(1)}, u32[]{:S(2)}, u32[]{:S(2)}) %collective-permute-start.34) | collective-permute-done | bytes 294944 | tf_op jit(solution)/shard_map/ppermute | solution.py:71
  150.2 13.4 %back_kernel.1 = (bf16[1024,576]{1,0:T(8,128)(2,1)S(1)}, f32[3,5,128,128]{3,2,1,0:T(8,128)S(1)}, f32[1024,768]{1,0:T(8,128)S(1)}) custom-call(s32[21]{0:T(128)S(1)} %copy-done, bf16[1024,576]{1,0:T(8,128)(2,1)S(1)} %get-tuple-element.208.qkv_ref, f32[8,128]{1,0:T(8,128)S(1)} %get-tuple-element.161.refs_9_.info_ref.refs_0_, ...), custom_call_target="tpu_custom_call" | custom-call | flops 2000000000 | bytes 8388608 | tf_op jit(solution)/shard_map/back_kernel/pallas_call | solution.py:157
  170.4 2.6 collective-permute-start.42
  176.8 3.5 %collective-permute-done.40.refs_8_ = bf16[256,768]{1,0:T(8,128)(2,1)S(1)} collective-permute-done((bf16[256,768]{1,0:T(8,128)(2,1)S(1)}, bf16[256,768]{1,0:T(8,128)(2,1)S(1)}, u32[]{:S(2)}, u32[]{:S(2)}) %collective-permute-start.40) | collective-permute-done | bytes 393248 | tf_op jit(solution)/shard_map/ppermute | solution.py:66
  191.0 2.8 sums_kernel.1.refs_2_.refs_4_
  195.3 3.9 %collective-permute-done.47.refs_4_ = bf16[2,96,768]{2,1,0:T(8,128)(2,1)S(1)} collective-permute-done((bf16[2,96,768]{2,1,0:T(8,128)(2,1)S(1)}, bf16[2,96,768]{2,1,0:T(8,128)(2,1)S(1)}, u32[]{:S(2)}, u32[]{:S(2)}) %collective-permute-start.47) | collective-permute-done | bytes 294944 | tf_op jit(solution)/shard_map/ppermute | solution.py:71
  201.3 7.0 %collective-permute-start.50 = (bf16[2,24,768]{2,1,0:T(8,128)(2,1)S(1)}, bf16[2,24,768]{2,1,0:T(8,128)(2,1)S(1)}, u32[]{:S(2)}, u32[]{:S(2)}) collective-permute-start(bf16[2,24,768]{2,1,0:T(8,128)(2,1)S(1)} %get-tuple-element.258), channel_id=1, source_target_pairs={{0,2},{1,3},{2,0},{3,1},{4,6},{5,7},{6,4},{7,5},{8,10},{9,11},{10,... | collective-permute-start | bytes 221192 | tf_op jit(solution)/shard_map/ppermute | solution.py:66
  211.3 3.5 %collective-permute-done.44.refs_1_ = bf16[2,128,768]{2,1,0:T(8,128)(2,1)S(1)} collective-permute-done((bf16[2,128,768]{2,1,0:T(8,128)(2,1)S(1)}, bf16[2,128,768]{2,1,0:T(8,128)(2,1)S(1)}, u32[]{:S(2)}, u32[]{:S(2)}) %collective-permute-start.44) | collective-permute-done | bytes 393248 | tf_op jit(solution)/shard_map/ppermute | solution.py:827
  218.4 8.3 %collective-permute-done.52.refs_1_ = bf16[3,24,768]{2,1,0:T(8,128)(2,1)S(1)} collective-permute-done((bf16[3,24,768]{2,1,0:T(8,128)(2,1)S(1)}, bf16[3,24,768]{2,1,0:T(8,128)(2,1)S(1)}, u32[]{:S(2)}, u32[]{:S(2)}) %collective-permute-start.52) | collective-permute-done | bytes 110624 | tf_op jit(solution)/shard_map/ppermute | solution.py:71
  227.4 4.1 %collective-permute-done.53.refs_1_ = bf16[6,24,768]{2,1,0:T(8,128)(2,1)S(1)} collective-permute-done((bf16[6,24,768]{2,1,0:T(8,128)(2,1)S(1)}, bf16[6,24,768]{2,1,0:T(8,128)(2,1)S(1)}, u32[]{:S(2)}, u32[]{:S(2)}) %collective-permute-start.53) | collective-permute-done | bytes 221216 | tf_op jit(solution)/shard_map/ppermute | solution.py:71
  235.6 2.7 collective-permute-done.56.refs_2_
  239.0 3.0 %collective-permute-start.59 = (bf16[3,24,768]{2,1,0:T(8,128)(2,1)S(1)}, bf16[3,24,768]{2,1,0:T(8,128)(2,1)S(1)}, u32[]{:S(2)}, u32[]{:S(2)}) collective-permute-start(bf16[3,24,768]{2,1,0:T(8,128)(2,1)S(1)} %qkv_collect.1.refs_0_), channel_id=1, source_target_pairs={{0,16},{4,20},{8,24},{12,28},{16,0},{20,4},{24,8},{28,12},{1,17},{... | collective-permute-start | bytes 331784 | tf_op jit(solution)/shard_map/ppermute | solution.py:71
  242.0 5.9 %collective-permute-done.58.refs_1_ = bf16[11,24,768]{2,1,0:T(8,128)(2,1)S(1)} collective-permute-done((bf16[11,24,768]{2,1,0:T(8,128)(2,1)S(1)}, bf16[11,24,768]{2,1,0:T(8,128)(2,1)S(1)}, u32[]{:S(2)}, u32[]{:S(2)}) %collective-permute-start.58) | collective-permute-done | bytes 405536 | tf_op jit(solution)/shard_map/ppermute | solution.py:71
  250.4 6.9 %collective-permute-done.60.refs_1_ = bf16[6,24,768]{2,1,0:T(8,128)(2,1)S(1)} collective-permute-done((bf16[6,24,768]{2,1,0:T(8,128)(2,1)S(1)}, bf16[6,24,768]{2,1,0:T(8,128)(2,1)S(1)}, u32[]{:S(2)}, u32[]{:S(2)}) %collective-permute-start.60) | collective-permute-done | bytes 221216 | tf_op jit(solution)/shard_map/ppermute | solution.py:71
  260.6 8.1 %collective-permute-done.61.refs_2_ = bf16[21,24,768]{2,1,0:T(8,128)(2,1)S(1)} collective-permute-done((bf16[21,24,768]{2,1,0:T(8,128)(2,1)S(1)}, bf16[21,24,768]{2,1,0:T(8,128)(2,1)S(1)}, u32[]{:S(2)}, u32[]{:S(2)}) %collective-permute-start.61) | collective-permute-done | bytes 774176 | tf_op jit(solution)/shard_map/ppermute | solution.py:71
  268.7 2.4 inner_rows.1
  271.1 4.4 %collective-permute-done.43.refs_0_ = bf16[2,128,768]{2,1,0:T(8,128)(2,1)S(1)} collective-permute-done((bf16[2,128,768]{2,1,0:T(8,128)(2,1)S(1)}, bf16[2,128,768]{2,1,0:T(8,128)(2,1)S(1)}, u32[]{:S(2)}, u32[]{:S(2)}) %collective-permute-start.43) | collective-permute-done | bytes 393248 | tf_op jit(solution)/shard_map/ppermute | solution.py:826
  (147 shorter events, 102.3 us)
Async XLA Ops:
  4.8 20.2 %collective-permute-start = (bf16[208,576]{1,0:T(8,128)(2,1)}, bf16[208,576]{1,0:T(8,128)(2,1)S(1)}, u32[]{:S(2)}, u32[]{:S(2)}) collective-permute-start(bf16[208,576]{1,0:T(8,128)(2,1)} %get-tuple-element.152), channel_id=1, source_target_pairs={{0,1},{1,0},{2,3},{3,2},{4,5},{5,4},{6,7},{7,6},{8,9},{9,8},{10,11... | collective-permute-start | bytes 718856 | tf_op jit(solution)/shard_map/ppermute | solution.py:66
  4.9 20.1 %collective-permute-start.1 = (bf16[208,576]{1,0:T(8,128)(2,1)}, bf16[208,576]{1,0:T(8,128)(2,1)S(1)}, u32[]{:S(2)}, u32[]{:S(2)}) collective-permute-start(bf16[208,576]{1,0:T(8,128)(2,1)} %get-tuple-element.153), channel_id=1, source_target_pairs={{0,2},{1,3},{2,0},{3,1},{4,6},{5,7},{6,4},{7,5},{8,10},{9,11},{10,... | collective-permute-start | bytes 718856 | tf_op jit(solution)/shard_map/ppermute | solution.py:66
  5.0 22.6 %collective-permute-start.2 = (bf16[208,576]{1,0:T(8,128)(2,1)}, bf16[208,576]{1,0:T(8,128)(2,1)S(1)}, u32[]{:S(2)}, u32[]{:S(2)}) collective-permute-start(bf16[208,576]{1,0:T(8,128)(2,1)} %get-tuple-element.154), channel_id=1, source_target_pairs={{0,3},{1,2},{2,1},{3,0},{4,7},{5,6},{6,5},{7,4},{8,11},{9,10},{10,... | collective-permute-start | bytes 718856 | tf_op jit(solution)/shard_map/ppermute | solution.py:66
  6.8 15.6 %collective-permute-start.4 = (bf16[128,768]{1,0:T(8,128)(2,1)}, bf16[128,768]{1,0:T(8,128)(2,1)S(1)}, u32[]{:S(2)}, u32[]{:S(2)}) collective-permute-start(bf16[128,768]{1,0:T(8,128)(2,1)} %get-tuple-element.157), channel_id=1, source_target_pairs={{0,4},{1,20},{2,12},{3,28},{4,0},{5,16},{6,8},{7,24},{8,6},{9,22},... | collective-permute-start | bytes 589832 | tf_op jit(solution)/shard_map/ppermute | solution.py:823
  9.2 15.8 %collective-permute-start.3 = (bf16[128,768]{1,0:T(8,128)(2,1)}, bf16[128,768]{1,0:T(8,128)(2,1)S(1)}, u32[]{:S(2)}, u32[]{:S(2)}) collective-permute-start(bf16[128,768]{1,0:T(8,128)(2,1)} %get-tuple-element.156), channel_id=1, source_target_pairs={{0,0},{1,16},{2,8},{3,24},{4,4},{5,20},{6,12},{7,28},{8,2},{9,18},... | collective-permute-start | bytes 589832 | tf_op jit(solution)/shard_map/ppermute | solution.py:823
  25.0 11.5 %collective-permute-start.5 = (bf16[128,768]{1,0:T(8,128)(2,1)S(1)}, bf16[128,768]{1,0:T(8,128)(2,1)S(1)}, u32[]{:S(2)}, u32[]{:S(2)}) collective-permute-start(bf16[128,768]{1,0:T(8,128)(2,1)S(1)} %collective-permute-done.3.refs_0_.near_ref.refs_1_), channel_id=1, source_target_pairs={{0,2},{1,3},{2,0},{3,1},{4,6},{5,7},{6,4},{7,5},{8,10},{9,11},{10,... | collective-permute-start | bytes 589832 | tf_op jit(solution)/shard_map/ppermute | solution.py:66
  25.0 12.7 %collective-permute-start.7 = (bf16[128,768]{1,0:T(8,128)(2,1)S(1)}, bf16[128,768]{1,0:T(8,128)(2,1)S(1)}, u32[]{:S(2)}, u32[]{:S(2)}) collective-permute-start(bf16[128,768]{1,0:T(8,128)(2,1)S(1)} %collective-permute-done.3.refs_0_.near_ref.refs_1_), channel_id=1, source_target_pairs={{0,1},{1,0},{2,3},{3,2},{4,5},{5,4},{6,7},{7,6},{8,9},{9,8},{10,11... | collective-permute-start | bytes 589832 | tf_op jit(solution)/shard_map/ppermute | solution.py:66
  25.0 15.2 %collective-permute-start.8 = (bf16[128,768]{1,0:T(8,128)(2,1)S(1)}, bf16[128,768]{1,0:T(8,128)(2,1)S(1)}, u32[]{:S(2)}, u32[]{:S(2)}) collective-permute-start(bf16[128,768]{1,0:T(8,128)(2,1)S(1)} %collective-permute-done.4.refs_1_.far_ref.refs_2_), channel_id=1, source_target_pairs={{0,1},{1,0},{2,3},{3,2},{4,5},{5,4},{6,7},{7,6},{8,9},{9,8},{10,11... | collective-permute-start | bytes 589832 | tf_op jit(solution)/shard_map/ppermute | solution.py:66
  37.6 18.2 %collective-permute-start.11 = (bf16[2,96,768]{2,1,0:T(8,128)(2,1)S(1)}, bf16[2,96,768]{2,1,0:T(8,128)(2,1)S(1)}, u32[]{:S(2)}, u32[]{:S(2)}) collective-permute-start(bf16[2,96,768]{2,1,0:T(8,128)(2,1)S(1)} %get-tuple-element.166), channel_id=1, source_target_pairs={{0,2},{1,3},{2,0},{3,1},{4,6},{5,7},{6,4},{7,5},{8,10},{9,11},{10,... | collective-permute-start | bytes 884744 | tf_op jit(solution)/shard_map/ppermute | solution.py:66
  37.7 16.0 %collective-permute-start.13 = (bf16[128,768]{1,0:T(8,128)(2,1)S(1)}, bf16[128,768]{1,0:T(8,128)(2,1)S(1)}, u32[]{:S(2)}, u32[]{:S(2)}) collective-permute-start(bf16[128,768]{1,0:T(8,128)(2,1)S(1)} %get-tuple-element.170), channel_id=1, source_target_pairs={{0,4},{1,20},{2,12},{3,28},{4,0},{5,16},{6,8},{7,24},{8,6},{9,22},... | collective-permute-start | bytes 589832 | tf_op jit(solution)/shard_map/ppermute | solution.py:823
  40.2 15.6 %collective-permute-start.12 = (bf16[128,768]{1,0:T(8,128)(2,1)S(1)}, bf16[128,768]{1,0:T(8,128)(2,1)S(1)}, u32[]{:S(2)}, u32[]{:S(2)}) collective-permute-start(bf16[128,768]{1,0:T(8,128)(2,1)S(1)} %get-tuple-element.168), channel_id=1, source_target_pairs={{0,0},{1,16},{2,8},{3,24},{4,4},{5,20},{6,12},{7,28},{8,2},{9,18},... | collective-permute-start | bytes 589832 | tf_op jit(solution)/shard_map/ppermute | solution.py:823
  59.5 12.0 %collective-permute-start.19 = (bf16[2,96,768]{2,1,0:T(8,128)(2,1)S(1)}, bf16[2,96,768]{2,1,0:T(8,128)(2,1)S(1)}, u32[]{:S(2)}, u32[]{:S(2)}) collective-permute-start(bf16[2,96,768]{2,1,0:T(8,128)(2,1)S(1)} %collective-permute-done.11.y_ref), channel_id=1, source_target_pairs={{0,4},{4,0},{8,12},{12,8},{16,20},{20,16},{24,28},{28,24},{1,5},{5... | collective-permute-start | bytes 884744 | tf_op jit(solution)/shard_map/ppermute | solution.py:71
  60.9 11.5 %collective-permute-start.20 = (bf16[2,96,768]{2,1,0:T(8,128)(2,1)S(1)}, bf16[2,96,768]{2,1,0:T(8,128)(2,1)S(1)}, u32[]{:S(2)}, u32[]{:S(2)}) collective-permute-start(bf16[2,96,768]{2,1,0:T(8,128)(2,1)S(1)} %collective-permute-done.11.y_ref), channel_id=1, source_target_pairs={{0,1},{1,0},{2,3},{3,2},{4,5},{5,4},{6,7},{7,6},{8,9},{9,8},{10,11... | collective-permute-start | bytes 884744 | tf_op jit(solution)/shard_map/ppermute | solution.py:66
  60.9 11.5 %collective-permute-start.18 = (bf16[192,768]{1,0:T(8,128)(2,1)S(1)}, bf16[192,768]{1,0:T(8,128)(2,1)S(1)}, u32[]{:S(2)}, u32[]{:S(2)}) collective-permute-start(bf16[192,768]{1,0:T(8,128)(2,1)S(1)} %get-tuple-element.177), channel_id=1, source_target_pairs={{0,1},{1,0},{2,3},{3,2},{4,5},{5,4},{6,7},{7,6},{8,9},{9,8},{10,11... | collective-permute-start | bytes 884744 | tf_op jit(solution)/shard_map/ppermute | solution.py:66
  102.1 11.5 %collective-permute-start.27 = (bf16[256,768]{1,0:T(8,128)(2,1)S(1)}, bf16[256,768]{1,0:T(8,128)(2,1)S(1)}, u32[]{:S(2)}, u32[]{:S(2)}) collective-permute-start(bf16[256,768]{1,0:T(8,128)(2,1)S(1)} %get-tuple-element.188.own_ref), channel_id=1, source_target_pairs={{0,2},{1,3},{2,0},{3,1},{4,6},{5,7},{6,4},{7,5},{8,10},{9,11},{10,... | collective-permute-start | bytes 1179656 | tf_op jit(solution)/shard_map/ppermute | solution.py:66
  119.4 15.4 %collective-permute-start.33 = (bf16[4,96,768]{2,1,0:T(8,128)(2,1)S(1)}, bf16[4,96,768]{2,1,0:T(8,128)(2,1)S(1)}, u32[]{:S(2)}, u32[]{:S(2)}) collective-permute-start(bf16[4,96,768]{2,1,0:T(8,128)(2,1)S(1)} %get-tuple-element.196), channel_id=1, source_target_pairs={{0,4},{4,0},{8,12},{12,8},{16,20},{20,16},{24,28},{28,24},{1,5},{5... | collective-permute-start | bytes 1769480 | tf_op jit(solution)/shard_map/ppermute | solution.py:71
  146.7 18.6 %collective-permute-start.38 = (bf16[20,24,768]{2,1,0:T(8,128)(2,1)S(1)}, bf16[20,24,768]{2,1,0:T(8,128)(2,1)S(1)}, u32[]{:S(2)}, u32[]{:S(2)}) collective-permute-start(bf16[20,24,768]{2,1,0:T(8,128)(2,1)S(1)} %get-tuple-element.223), channel_id=1, source_target_pairs={{0,4},{4,0},{8,12},{12,8},{16,20},{20,16},{24,28},{28,24},{1,5},{5... | collective-permute-start | bytes 2211848 | tf_op jit(solution)/shard_map/ppermute | solution.py:71
  148.2 15.3 %collective-permute-start.37 = (bf16[1,96,768]{2,1,0:T(8,128)(2,1)S(1)}, bf16[1,96,768]{2,1,0:T(8,128)(2,1)S(1)}, u32[]{:S(2)}, u32[]{:S(2)}) collective-permute-start(bf16[1,96,768]{2,1,0:T(8,128)(2,1)S(1)} %get-tuple-element.221), channel_id=1, source_target_pairs={{0,16},{4,20},{8,24},{12,28},{16,0},{20,4},{24,8},{28,12},{1,17},{... | collective-permute-start | bytes 442376 | tf_op jit(solution)/shard_map/ppermute | solution.py:71
  169.6 13.5 %collective-permute-start.41 = (bf16[10,24,768]{2,1,0:T(8,128)(2,1)S(1)}, bf16[10,24,768]{2,1,0:T(8,128)(2,1)S(1)}, u32[]{:S(2)}, u32[]{:S(2)}) collective-permute-start(bf16[10,24,768]{2,1,0:T(8,128)(2,1)S(1)} %get-tuple-element.235), channel_id=1, source_target_pairs={{0,8},{4,12},{8,0},{12,4},{16,24},{20,28},{24,16},{28,20},{1,9},{5... | collective-permute-start | bytes 1105928 | tf_op jit(solution)/shard_map/ppermute | solution.py:71
  175.1 14.9 %collective-permute-start.45 = (bf16[12,24,768]{2,1,0:T(8,128)(2,1)S(1)}, bf16[12,24,768]{2,1,0:T(8,128)(2,1)S(1)}, u32[]{:S(2)}, u32[]{:S(2)}) collective-permute-start(bf16[12,24,768]{2,1,0:T(8,128)(2,1)S(1)} %get-tuple-element.231), channel_id=1, source_target_pairs={{0,4},{4,0},{8,12},{12,8},{16,20},{20,16},{24,28},{28,24},{1,5},{5... | collective-permute-start | bytes 1327112 | tf_op jit(solution)/shard_map/ppermute | solution.py:71
  186.6 12.6 %collective-permute-start.47 = (bf16[2,96,768]{2,1,0:T(8,128)(2,1)S(1)}, bf16[2,96,768]{2,1,0:T(8,128)(2,1)S(1)}, u32[]{:S(2)}, u32[]{:S(2)}) collective-permute-start(bf16[2,96,768]{2,1,0:T(8,128)(2,1)S(1)} %get-tuple-element.251.refs_3_), channel_id=1, source_target_pairs={{0,8},{4,12},{8,0},{12,4},{16,24},{20,28},{24,16},{28,20},{1,9},{5... | collective-permute-start | bytes 884744 | tf_op jit(solution)/shard_map/ppermute | solution.py:71
  188.3 26.5 %collective-permute-start.44 = (bf16[2,128,768]{2,1,0:T(8,128)(2,1)S(1)}, bf16[2,128,768]{2,1,0:T(8,128)(2,1)S(1)}, u32[]{:S(2)}, u32[]{:S(2)}) collective-permute-start(bf16[2,128,768]{2,1,0:T(8,128)(2,1)S(1)} %get-tuple-element.240), channel_id=1, source_target_pairs={{4,0},{20,1},{12,2},{28,3},{0,4},{16,5},{8,6},{24,7},{6,8},{22,9},... | collective-permute-start | bytes 1179656 | tf_op jit(solution)/shard_map/ppermute | solution.py:827
  190.7 18.7 %collective-permute-start.48 = (bf16[6,24,768]{2,1,0:T(8,128)(2,1)S(1)}, bf16[6,24,768]{2,1,0:T(8,128)(2,1)S(1)}, u32[]{:S(2)}, u32[]{:S(2)}) collective-permute-start(bf16[6,24,768]{2,1,0:T(8,128)(2,1)S(1)} %get-tuple-element.246), channel_id=1, source_target_pairs={{0,8},{4,12},{8,0},{12,4},{16,24},{20,28},{24,16},{28,20},{1,9},{5... | collective-permute-start | bytes 663560 | tf_op jit(solution)/shard_map/ppermute | solution.py:71
  199.9 31.6 %collective-permute-start.54 = (bf16[4,96,768]{2,1,0:T(8,128)(2,1)S(1)}, bf16[4,96,768]{2,1,0:T(8,128)(2,1)S(1)}, u32[]{:S(2)}, u32[]{:S(2)}) collective-permute-start(bf16[4,96,768]{2,1,0:T(8,128)(2,1)S(1)} %get-tuple-element.252.refs_3_), channel_id=1, source_target_pairs={{0,4},{4,0},{8,12},{12,8},{16,20},{20,16},{24,28},{28,24},{1,5},{5... | collective-permute-start | bytes 1769480 | tf_op jit(solution)/shard_map/ppermute | solution.py:71
  201.3 13.4 %collective-permute-start.49 = (bf16[2,24,768]{2,1,0:T(8,128)(2,1)S(1)}, bf16[2,24,768]{2,1,0:T(8,128)(2,1)S(1)}, u32[]{:S(2)}, u32[]{:S(2)}) collective-permute-start(bf16[2,24,768]{2,1,0:T(8,128)(2,1)S(1)} %get-tuple-element.257), channel_id=1, source_target_pairs={{0,1},{1,0},{2,3},{3,2},{4,5},{5,4},{6,7},{7,6},{8,9},{9,8},{10,11... | collective-permute-start | bytes 221192 | tf_op jit(solution)/shard_map/ppermute | solution.py:66
  201.3 14.2 %collective-permute-start.50 = (bf16[2,24,768]{2,1,0:T(8,128)(2,1)S(1)}, bf16[2,24,768]{2,1,0:T(8,128)(2,1)S(1)}, u32[]{:S(2)}, u32[]{:S(2)}) collective-permute-start(bf16[2,24,768]{2,1,0:T(8,128)(2,1)S(1)} %get-tuple-element.258), channel_id=1, source_target_pairs={{0,2},{1,3},{2,0},{3,1},{4,6},{5,7},{6,4},{7,5},{8,10},{9,11},{10,... | collective-permute-start | bytes 221192 | tf_op jit(solution)/shard_map/ppermute | solution.py:66
  214.8 11.9 %collective-permute-start.52 = (bf16[3,24,768]{2,1,0:T(8,128)(2,1)S(1)}, bf16[3,24,768]{2,1,0:T(8,128)(2,1)S(1)}, u32[]{:S(2)}, u32[]{:S(2)}) collective-permute-start(bf16[3,24,768]{2,1,0:T(8,128)(2,1)S(1)} %get-tuple-element.262), channel_id=1, source_target_pairs={{0,16},{4,20},{8,24},{12,28},{16,0},{20,4},{24,8},{28,12},{1,17},{... | collective-permute-start | bytes 331784 | tf_op jit(solution)/shard_map/ppermute | solution.py:71
  216.9 14.6 %collective-permute-start.53 = (bf16[6,24,768]{2,1,0:T(8,128)(2,1)S(1)}, bf16[6,24,768]{2,1,0:T(8,128)(2,1)S(1)}, u32[]{:S(2)}, u32[]{:S(2)}) collective-permute-start(bf16[6,24,768]{2,1,0:T(8,128)(2,1)S(1)} %get-tuple-element.264.refs_0_), channel_id=1, source_target_pairs={{0,16},{4,20},{8,24},{12,28},{16,0},{20,4},{24,8},{28,12},{1,17},{... | collective-permute-start | bytes 663560 | tf_op jit(solution)/shard_map/ppermute | solution.py:71
  233.6 14.3 %collective-permute-start.58 = (bf16[11,24,768]{2,1,0:T(8,128)(2,1)S(1)}, bf16[11,24,768]{2,1,0:T(8,128)(2,1)S(1)}, u32[]{:S(2)}, u32[]{:S(2)}) collective-permute-start(bf16[11,24,768]{2,1,0:T(8,128)(2,1)S(1)} %get-tuple-element.271.refs_0_), channel_id=1, source_target_pairs={{0,8},{4,12},{8,0},{12,4},{16,24},{20,28},{24,16},{28,20},{1,9},{5... | collective-permute-start | bytes 1216520 | tf_op jit(solution)/shard_map/ppermute | solution.py:71
  248.5 20.2 %collective-permute-start.61 = (bf16[21,24,768]{2,1,0:T(8,128)(2,1)S(1)}, bf16[21,24,768]{2,1,0:T(8,128)(2,1)S(1)}, u32[]{:S(2)}, u32[]{:S(2)}) collective-permute-start(bf16[21,24,768]{2,1,0:T(8,128)(2,1)S(1)} %get-tuple-element.275.refs_1_), channel_id=1, source_target_pairs={{0,4},{4,0},{8,12},{12,8},{16,20},{20,16},{24,28},{28,24},{1,5},{5... | collective-permute-start | bytes 2322440 | tf_op jit(solution)/shard_map/ppermute | solution.py:71
  257.8 19.2 %collective-permute-start.62 = (bf16[12,24,768]{2,1,0:T(8,128)(2,1)S(1)}, bf16[12,24,768]{2,1,0:T(8,128)(2,1)S(1)}, u32[]{:S(2)}, u32[]{:S(2)}) collective-permute-start(bf16[12,24,768]{2,1,0:T(8,128)(2,1)S(1)} %qkv_low.1.refs_2_), channel_id=1, source_target_pairs={{0,4},{4,0},{8,12},{12,8},{16,20},{20,16},{24,28},{28,24},{1,5},{5... | collective-permute-start | bytes 1327112 | tf_op jit(solution)/shard_map/ppermute | solution.py:71
  258.7 16.7 %collective-permute-start.43 = (bf16[2,128,768]{2,1,0:T(8,128)(2,1)S(1)}, bf16[2,128,768]{2,1,0:T(8,128)(2,1)S(1)}, u32[]{:S(2)}, u32[]{:S(2)}) collective-permute-start(bf16[2,128,768]{2,1,0:T(8,128)(2,1)S(1)} %get-tuple-element.239), channel_id=1, source_target_pairs={{0,0},{16,1},{8,2},{24,3},{4,4},{20,5},{12,6},{28,7},{2,8},{18,9},... | collective-permute-start | bytes 1179656 | tf_op jit(solution)/shard_map/ppermute | solution.py:826
  (37 other events, 249.3 us)

commit v2 on v1

--- a/solution.py
+++ b/solution.py
@@ -334,7 +334,7 @@
 def front_kernel(here, small_ref, *refs):
     pieces, (w_ref, info_ref, bias_ref, out_w_ref), (normed_ref, qkv_ref) = refs[:8], refs[8:12], refs[12:14]
     project(here, small_ref, pieces, w_ref, normed_ref, qkv_ref)
-    attention_kernel(512, (COLS, 2 * COLS), here, qkv_ref, qkv_ref, info_ref, bias_ref, out_w_ref, *refs[14:])
+    attention_kernel(GROUP, (COLS, 2 * COLS), here, qkv_ref, qkv_ref, info_ref, bias_ref, out_w_ref, *refs[14:])
 
 
 def attend_back(
@@ -885,7 +885,7 @@
             front_kernel,
             proj_shapes + attn_shapes,
             (here, small) + pieces + (w_qkv, info, bias, w_out),
-            scratch=attn_scratch(GROUP, 512),
+            scratch=attn_scratch(GROUP, GROUP),
             mib=14,
         )
     else:
@@ -1114,7 +1114,7 @@
             (
                 inner_collect,
                 (parts_of(TP + 1 + 1), sums_shape),
-                (after(inner_blocks[0], qkv_keep, home_far),) + inner_blocks[1:] + (sums,),
+                (after(inner_blocks[0], qkv_keep),) + inner_blocks[1:] + (sums,),
             ),
         )
         inner_came = to_ctx(inner_chunk, 4)
@@ -1127,7 +1127,7 @@
             (
                 inner_high,
                 (parts_of(2 * TP + 2 + 1), sums_shape),
-                (after(inner_chunk, qkv_blocks[0]), inner_came, sums),
+                (after(inner_chunk, qkv_blocks[0], home_far), inner_came, sums),
             ),
             (outer_rows, (shape(D, D),), (outer_half, outer_came)),
         )

time: 283 us -> 282 us (level)
  waiting for transfers between devices: 150 us -> 146 us
  starting transfers between devices: 56.8 us -> 60.6 us
    ppermute x1, waiting for transfers between devices: 3.52 us -> 0.01 us  [from_home(): far = lax.ppermute(far, AXES, backwards(cross))]
    ppermute x19, starting transfers between devices: 23.5 us -> 26.7 us  [to_ctx(): return lax.ppermute(value, 'ctx', [(i, i ^ offset) for i in range(n_ctx)])]
    ppermute x19, waiting for transfers between devices: 54.9 us -> 51.7 us  [to_ctx(): return lax.ppermute(value, 'ctx', [(i, i ^ offset) for i in range(n_ctx)])]
  transfers between devices with their start and end apart: 63 -> 63, of which waited for: 40 -> 39; matrix products, arithmetic and copies ran while one was open for 0% -> 0% of each run, Pallas kernels for 18% -> 18%
where the time goes in v2:
time: 282 us; the launch traced here: 279 us
  waiting for transfers between devices  146 us (52%)
  Pallas kernels  69.3 us (25%)
  starting transfers between devices  60.6 us (21%)
    ppermute x38, waiting for transfers between devices, to_partner(): return lax.ppermute(value, 'wsh', [(i, i ^ offset) for i in range(TP)])  72.6 us
    pallas_call x40, Pallas kernels, call(): pl.pallas_call(body, name=name_of(body), out_shape=tuple(outs), in_specs=...  69.3 us
    ppermute x19, waiting for transfers between devices, to_ctx(): return lax.ppermute(value, 'ctx', [(i, i ^ offset) for i in range(n_ctx)])  51.7 us
    ppermute x19, starting transfers between devices, to_ctx(): return lax.ppermute(value, 'ctx', [(i, i ^ offset) for i in range(n_ctx)])  26.7 us
    ppermute x38, starting transfers between devices, to_partner(): return lax.ppermute(value, 'wsh', [(i, i ^ offset) for i in range(TP)])  18 us
    ppermute x2, waiting for transfers between devices, to_home(): lax.ppermute(pair[1], AXES, cross)  11.2 us
    ppermute x2, starting transfers between devices, to_home(): lax.ppermute(pair[0], AXES, same)  6.77 us
    ppermute x1, waiting for transfers between devices, from_home(): near = lax.ppermute(near, AXES, backwards(same))  5.73 us
  transfers between devices with their start and end apart: 63, of which 39 were waited for; matrix products, arithmetic and copies ran while one was open for 0% of the time, Pallas kernels for 18%

profile of v2, /device:TPU:4, one launch (start us, length us, event | category | flops | bytes accessed | tf_op | source)
XLA Modules:
  0.0 278.7 jit_solution(17151993544345262745)
XLA Ops:
  1.3 3.5 %start_kernel.1 = (bf16[128,768]{1,0:T(8,128)(2,1)}, bf16[128,768]{1,0:T(8,128)(2,1)}, bf16[208,576]{1,0:T(8,128)(2,1)}, bf16[208,576]{1,0:T(8,128)(2,1)}, bf16[...) custom-call(s32[21]{0:T(128)} %stack.60.here, bf16[2,128,768]{2,1,0:T(8,128)(2,1)} %x_hbm.1, bf16[192,768]{1,0:T(8,128)(2,1)} %wq_hbm.1, ...), custom_call_target="tpu_custom_call" | custom-call | flops 2000000000 | bytes 8388608 | tf_op jit(solution)/shard_map/start_kernel/pallas_call | solution.py:157
  6.8 2.5 collective-permute-start.4
  9.2 3.3 %collective-permute-start.3 = (bf16[128,768]{1,0:T(8,128)(2,1)}, bf16[128,768]{1,0:T(8,128)(2,1)S(1)}, u32[]{:S(2)}, u32[]{:S(2)}) collective-permute-start(bf16[128,768]{1,0:T(8,128)(2,1)} %get-tuple-element.156), channel_id=1, source_target_pairs={{0,0},{1,16},{2,8},{3,24},{4,4},{5,20},{6,12},{7,28},{8,2},{9,18},... | collective-permute-start | bytes 589832 | tf_op jit(solution)/shard_map/ppermute | solution.py:823
  12.5 9.8 %collective-permute-done.4.refs_1_.far_ref.refs_2_ = bf16[128,768]{1,0:T(8,128)(2,1)S(1)} collective-permute-done((bf16[128,768]{1,0:T(8,128)(2,1)}, bf16[128,768]{1,0:T(8,128)(2,1)S(1)}, u32[]{:S(2)}, u32[]{:S(2)}) %collective-permute-start.4) | collective-permute-done | bytes 196640 | tf_op jit(solution)/shard_map/ppermute | solution.py:823
  22.3 2.6 collective-permute-done.3.refs_0_.near_ref.refs_1_
  30.1 2.6 collective-permute-done.6.refs_3_
  32.7 3.8 %collective-permute-done.5.refs_2_ = bf16[128,768]{1,0:T(8,128)(2,1)S(1)} collective-permute-done((bf16[128,768]{1,0:T(8,128)(2,1)S(1)}, bf16[128,768]{1,0:T(8,128)(2,1)S(1)}, u32[]{:S(2)}, u32[]{:S(2)}) %collective-permute-start.5) | collective-permute-done | bytes 196640 | tf_op jit(solution)/shard_map/ppermute | solution.py:66
  37.7 2.5 collective-permute-start.13
  40.2 3.5 %collective-permute-start.12 = (bf16[128,768]{1,0:T(8,128)(2,1)S(1)}, bf16[128,768]{1,0:T(8,128)(2,1)S(1)}, u32[]{:S(2)}, u32[]{:S(2)}) collective-permute-start(bf16[128,768]{1,0:T(8,128)(2,1)S(1)} %get-tuple-element.168), channel_id=1, source_target_pairs={{0,0},{1,16},{2,8},{3,24},{4,4},{5,20},{6,12},{7,28},{8,2},{9,18},... | collective-permute-start | bytes 589832 | tf_op jit(solution)/shard_map/ppermute | solution.py:823
  43.7 8.7 %front_kernel.1 = (bf16[1024,768]{1,0:T(8,128)(2,1)S(1)}, bf16[1024,576]{1,0:T(8,128)(2,1)S(1)}, f32[192,1024]{1,0:T(8,128)S(1)}, f32[8,1024]{1,0:T(8,128)S(1)}, f32[1024,768]{1,0:T(8,128)S(1)}) custom-call(s32[21]{0:T(128)S(1)} %copy-done, f32[4,16,576]{2,1,0:T(8,128)S(1)} %get-tuple-element.155.small_ref.refs_0_, ...), custom_call_target="tpu_custom_call" | custom-call | flops 2000000000 | bytes 8388608 | tf_op jit(solution)/shard_map/front_kernel/pallas_call | solution.py:157
  61.4 9.2 %collective-permute-done.15.y_ref = bf16[256,768]{1,0:T(8,128)(2,1)S(1)} collective-permute-done((bf16[256,768]{1,0:T(8,128)(2,1)S(1)}, bf16[256,768]{1,0:T(8,128)(2,1)S(1)}, u32[]{:S(2)}, u32[]{:S(2)}) %collective-permute-start.15) | collective-permute-done | bytes 393248 | tf_op jit(solution)/shard_map/ppermute | solution.py:66
  75.9 7.3 %collective-permute-done.17.own_ref.refs_2_ = bf16[256,768]{1,0:T(8,128)(2,1)S(1)} collective-permute-done((bf16[256,768]{1,0:T(8,128)(2,1)S(1)}, bf16[256,768]{1,0:T(8,128)(2,1)S(1)}, u32[]{:S(2)}, u32[]{:S(2)}) %collective-permute-start.17) | collective-permute-done | bytes 393248 | tf_op jit(solution)/shard_map/ppermute | solution.py:66
  89.8 10.9 %collective-permute-done.25.y_ref = bf16[256,768]{1,0:T(8,128)(2,1)S(1)} collective-permute-done((bf16[256,768]{1,0:T(8,128)(2,1)S(1)}, bf16[256,768]{1,0:T(8,128)(2,1)S(1)}, u32[]{:S(2)}, u32[]{:S(2)}) %collective-permute-start.25) | collective-permute-done | bytes 393248 | tf_op jit(solution)/shard_map/ppermute | solution.py:66
  107.1 6.5 %collective-permute-done.27.own_ref = bf16[256,768]{1,0:T(8,128)(2,1)S(1)} collective-permute-done((bf16[256,768]{1,0:T(8,128)(2,1)S(1)}, bf16[256,768]{1,0:T(8,128)(2,1)S(1)}, u32[]{:S(2)}, u32[]{:S(2)}) %collective-permute-start.27) | collective-permute-done | bytes 393248 | tf_op jit(solution)/shard_map/ppermute | solution.py:66
  123.8 8.6 %collective-permute-done.31.refs_5_ = bf16[256,768]{1,0:T(8,128)(2,1)S(1)} collective-permute-done((bf16[256,768]{1,0:T(8,128)(2,1)S(1)}, bf16[256,768]{1,0:T(8,128)(2,1)S(1)}, u32[]{:S(2)}, u32[]{:S(2)}) %collective-permute-start.31) | collective-permute-done | bytes 393248 | tf_op jit(solution)/shard_map/ppermute | solution.py:66
  135.6 8.1 %collective-permute-done.34.refs_8_ = bf16[2,96,768]{2,1,0:T(8,128)(2,1)S(1)} collective-permute-done((bf16[2,96,768]{2,1,0:T(8,128)(2,1)S(1)}, bf16[2,96,768]{2,1,0:T(8,128)(2,1)S(1)}, u32[]{:S(2)}, u32[]{:S(2)}) %collective-permute-start.34) | collective-permute-done | bytes 294944 | tf_op jit(solution)/shard_map/ppermute | solution.py:71
  150.2 13.4 %back_kernel.1 = (bf16[1024,576]{1,0:T(8,128)(2,1)S(1)}, f32[3,5,128,128]{3,2,1,0:T(8,128)S(1)}, f32[1024,768]{1,0:T(8,128)S(1)}) custom-call(s32[21]{0:T(128)S(1)} %copy-done, bf16[1024,576]{1,0:T(8,128)(2,1)S(1)} %get-tuple-element.208.qkv_ref, f32[8,128]{1,0:T(8,128)S(1)} %get-tuple-element.161.refs_9_.info_ref.refs_0_, ...), custom_call_target="tpu_custom_call" | custom-call | flops 2000000000 | bytes 8388608 | tf_op jit(solution)/shard_map/back_kernel/pallas_call | solution.py:157
  170.4 2.6 collective-permute-start.42
  176.8 3.5 %collective-permute-done.40.refs_8_ = bf16[256,768]{1,0:T(8,128)(2,1)S(1)} collective-permute-done((bf16[256,768]{1,0:T(8,128)(2,1)S(1)}, bf16[256,768]{1,0:T(8,128)(2,1)S(1)}, u32[]{:S(2)}, u32[]{:S(2)}) %collective-permute-start.40) | collective-permute-done | bytes 393248 | tf_op jit(solution)/shard_map/ppermute | solution.py:66
  191.0 2.8 sums_kernel.1.refs_2_.refs_4_
  195.3 3.9 %collective-permute-done.47.refs_4_ = bf16[2,96,768]{2,1,0:T(8,128)(2,1)S(1)} collective-permute-done((bf16[2,96,768]{2,1,0:T(8,128)(2,1)S(1)}, bf16[2,96,768]{2,1,0:T(8,128)(2,1)S(1)}, u32[]{:S(2)}, u32[]{:S(2)}) %collective-permute-start.47) | collective-permute-done | bytes 294944 | tf_op jit(solution)/shard_map/ppermute | solution.py:71
  201.3 7.0 %collective-permute-start.50 = (bf16[2,24,768]{2,1,0:T(8,128)(2,1)S(1)}, bf16[2,24,768]{2,1,0:T(8,128)(2,1)S(1)}, u32[]{:S(2)}, u32[]{:S(2)}) collective-permute-start(bf16[2,24,768]{2,1,0:T(8,128)(2,1)S(1)} %get-tuple-element.258), channel_id=1, source_target_pairs={{0,2},{1,3},{2,0},{3,1},{4,6},{5,7},{6,4},{7,5},{8,10},{9,11},{10,... | collective-permute-start | bytes 221192 | tf_op jit(solution)/shard_map/ppermute | solution.py:66
  211.3 3.2 %collective-permute-start.52 = (bf16[3,24,768]{2,1,0:T(8,128)(2,1)S(1)}, bf16[3,24,768]{2,1,0:T(8,128)(2,1)S(1)}, u32[]{:S(2)}, u32[]{:S(2)}) collective-permute-start(bf16[3,24,768]{2,1,0:T(8,128)(2,1)S(1)} %get-tuple-element.262), channel_id=1, source_target_pairs={{0,16},{4,20},{8,24},{12,28},{16,0},{20,4},{24,8},{28,12},{1,17},{... | collective-permute-start | bytes 331784 | tf_op jit(solution)/shard_map/ppermute | solution.py:71
  218.8 12.1 %collective-permute-done.53.refs_1_ = bf16[6,24,768]{2,1,0:T(8,128)(2,1)S(1)} collective-permute-done((bf16[6,24,768]{2,1,0:T(8,128)(2,1)S(1)}, bf16[6,24,768]{2,1,0:T(8,128)(2,1)S(1)}, u32[]{:S(2)}, u32[]{:S(2)}) %collective-permute-start.53) | collective-permute-done | bytes 221216 | tf_op jit(solution)/shard_map/ppermute | solution.py:71
  235.1 2.8 collective-permute-done.56.refs_2_
  238.9 3.1 %collective-permute-start.59 = (bf16[3,24,768]{2,1,0:T(8,128)(2,1)S(1)}, bf16[3,24,768]{2,1,0:T(8,128)(2,1)S(1)}, u32[]{:S(2)}, u32[]{:S(2)}) collective-permute-start(bf16[3,24,768]{2,1,0:T(8,128)(2,1)S(1)} %qkv_collect.1.refs_0_), channel_id=1, source_target_pairs={{0,16},{4,20},{8,24},{12,28},{16,0},{20,4},{24,8},{28,12},{1,17},{... | collective-permute-start | bytes 331784 | tf_op jit(solution)/shard_map/ppermute | solution.py:71
  242.0 5.1 %collective-permute-done.58.refs_1_ = bf16[11,24,768]{2,1,0:T(8,128)(2,1)S(1)} collective-permute-done((bf16[11,24,768]{2,1,0:T(8,128)(2,1)S(1)}, bf16[11,24,768]{2,1,0:T(8,128)(2,1)S(1)}, u32[]{:S(2)}, u32[]{:S(2)}) %collective-permute-start.58) | collective-permute-done | bytes 405536 | tf_op jit(solution)/shard_map/ppermute | solution.py:71
  249.8 7.2 %collective-permute-done.60.refs_1_ = bf16[6,24,768]{2,1,0:T(8,128)(2,1)S(1)} collective-permute-done((bf16[6,24,768]{2,1,0:T(8,128)(2,1)S(1)}, bf16[6,24,768]{2,1,0:T(8,128)(2,1)S(1)}, u32[]{:S(2)}, u32[]{:S(2)}) %collective-permute-start.60) | collective-permute-done | bytes 221216 | tf_op jit(solution)/shard_map/ppermute | solution.py:71
  258.4 2.4 collective-permute-start.43
  260.8 7.1 %collective-permute-done.61.refs_2_ = bf16[21,24,768]{2,1,0:T(8,128)(2,1)S(1)} collective-permute-done((bf16[21,24,768]{2,1,0:T(8,128)(2,1)S(1)}, bf16[21,24,768]{2,1,0:T(8,128)(2,1)S(1)}, u32[]{:S(2)}, u32[]{:S(2)}) %collective-permute-start.61) | collective-permute-done | bytes 774176 | tf_op jit(solution)/shard_map/ppermute | solution.py:71
  267.9 2.4 inner_rows.1
  270.2 5.7 %collective-permute-done.43.refs_0_ = bf16[2,128,768]{2,1,0:T(8,128)(2,1)S(1)} collective-permute-done((bf16[2,128,768]{2,1,0:T(8,128)(2,1)S(1)}, bf16[2,128,768]{2,1,0:T(8,128)(2,1)S(1)}, u32[]{:S(2)}, u32[]{:S(2)}) %collective-permute-start.43) | collective-permute-done | bytes 393248 | tf_op jit(solution)/shard_map/ppermute | solution.py:826
  (147 shorter events, 100.0 us)
Async XLA Ops:
  4.8 20.2 %collective-permute-start = (bf16[208,576]{1,0:T(8,128)(2,1)}, bf16[208,576]{1,0:T(8,128)(2,1)S(1)}, u32[]{:S(2)}, u32[]{:S(2)}) collective-permute-start(bf16[208,576]{1,0:T(8,128)(2,1)} %get-tuple-element.152), channel_id=1, source_target_pairs={{0,1},{1,0},{2,3},{3,2},{4,5},{5,4},{6,7},{7,6},{8,9},{9,8},{10,11... | collective-permute-start | bytes 718856 | tf_op jit(solution)/shard_map/ppermute | solution.py:66
  4.9 20.1 %collective-permute-start.1 = (bf16[208,576]{1,0:T(8,128)(2,1)}, bf16[208,576]{1,0:T(8,128)(2,1)S(1)}, u32[]{:S(2)}, u32[]{:S(2)}) collective-permute-start(bf16[208,576]{1,0:T(8,128)(2,1)} %get-tuple-element.153), channel_id=1, source_target_pairs={{0,2},{1,3},{2,0},{3,1},{4,6},{5,7},{6,4},{7,5},{8,10},{9,11},{10,... | collective-permute-start | bytes 718856 | tf_op jit(solution)/shard_map/ppermute | solution.py:66
  5.0 22.6 %collective-permute-start.2 = (bf16[208,576]{1,0:T(8,128)(2,1)}, bf16[208,576]{1,0:T(8,128)(2,1)S(1)}, u32[]{:S(2)}, u32[]{:S(2)}) collective-permute-start(bf16[208,576]{1,0:T(8,128)(2,1)} %get-tuple-element.154), channel_id=1, source_target_pairs={{0,3},{1,2},{2,1},{3,0},{4,7},{5,6},{6,5},{7,4},{8,11},{9,10},{10,... | collective-permute-start | bytes 718856 | tf_op jit(solution)/shard_map/ppermute | solution.py:66
  6.8 15.6 %collective-permute-start.4 = (bf16[128,768]{1,0:T(8,128)(2,1)}, bf16[128,768]{1,0:T(8,128)(2,1)S(1)}, u32[]{:S(2)}, u32[]{:S(2)}) collective-permute-start(bf16[128,768]{1,0:T(8,128)(2,1)} %get-tuple-element.157), channel_id=1, source_target_pairs={{0,4},{1,20},{2,12},{3,28},{4,0},{5,16},{6,8},{7,24},{8,6},{9,22},... | collective-permute-start | bytes 589832 | tf_op jit(solution)/shard_map/ppermute | solution.py:823
  9.2 15.8 %collective-permute-start.3 = (bf16[128,768]{1,0:T(8,128)(2,1)}, bf16[128,768]{1,0:T(8,128)(2,1)S(1)}, u32[]{:S(2)}, u32[]{:S(2)}) collective-permute-start(bf16[128,768]{1,0:T(8,128)(2,1)} %get-tuple-element.156), channel_id=1, source_target_pairs={{0,0},{1,16},{2,8},{3,24},{4,4},{5,20},{6,12},{7,28},{8,2},{9,18},... | collective-permute-start | bytes 589832 | tf_op jit(solution)/shard_map/ppermute | solution.py:823
  25.0 11.5 %collective-permute-start.5 = (bf16[128,768]{1,0:T(8,128)(2,1)S(1)}, bf16[128,768]{1,0:T(8,128)(2,1)S(1)}, u32[]{:S(2)}, u32[]{:S(2)}) collective-permute-start(bf16[128,768]{1,0:T(8,128)(2,1)S(1)} %collective-permute-done.3.refs_0_.near_ref.refs_1_), channel_id=1, source_target_pairs={{0,2},{1,3},{2,0},{3,1},{4,6},{5,7},{6,4},{7,5},{8,10},{9,11},{10,... | collective-permute-start | bytes 589832 | tf_op jit(solution)/shard_map/ppermute | solution.py:66
  25.0 12.7 %collective-permute-start.7 = (bf16[128,768]{1,0:T(8,128)(2,1)S(1)}, bf16[128,768]{1,0:T(8,128)(2,1)S(1)}, u32[]{:S(2)}, u32[]{:S(2)}) collective-permute-start(bf16[128,768]{1,0:T(8,128)(2,1)S(1)} %collective-permute-done.3.refs_0_.near_ref.refs_1_), channel_id=1, source_target_pairs={{0,1},{1,0},{2,3},{3,2},{4,5},{5,4},{6,7},{7,6},{8,9},{9,8},{10,11... | collective-permute-start | bytes 589832 | tf_op jit(solution)/shard_map/ppermute | solution.py:66
  25.0 15.2 %collective-permute-start.8 = (bf16[128,768]{1,0:T(8,128)(2,1)S(1)}, bf16[128,768]{1,0:T(8,128)(2,1)S(1)}, u32[]{:S(2)}, u32[]{:S(2)}) collective-permute-start(bf16[128,768]{1,0:T(8,128)(2,1)S(1)} %collective-permute-done.4.refs_1_.far_ref.refs_2_), channel_id=1, source_target_pairs={{0,1},{1,0},{2,3},{3,2},{4,5},{5,4},{6,7},{7,6},{8,9},{9,8},{10,11... | collective-permute-start | bytes 589832 | tf_op jit(solution)/shard_map/ppermute | solution.py:66
  37.6 18.2 %collective-permute-start.11 = (bf16[2,96,768]{2,1,0:T(8,128)(2,1)S(1)}, bf16[2,96,768]{2,1,0:T(8,128)(2,1)S(1)}, u32[]{:S(2)}, u32[]{:S(2)}) collective-permute-start(bf16[2,96,768]{2,1,0:T(8,128)(2,1)S(1)} %get-tuple-element.166), channel_id=1, source_target_pairs={{0,2},{1,3},{2,0},{3,1},{4,6},{5,7},{6,4},{7,5},{8,10},{9,11},{10,... | collective-permute-start | bytes 884744 | tf_op jit(solution)/shard_map/ppermute | solution.py:66
  37.7 16.0 %collective-permute-start.13 = (bf16[128,768]{1,0:T(8,128)(2,1)S(1)}, bf16[128,768]{1,0:T(8,128)(2,1)S(1)}, u32[]{:S(2)}, u32[]{:S(2)}) collective-permute-start(bf16[128,768]{1,0:T(8,128)(2,1)S(1)} %get-tuple-element.170), channel_id=1, source_target_pairs={{0,4},{1,20},{2,12},{3,28},{4,0},{5,16},{6,8},{7,24},{8,6},{9,22},... | collective-permute-start | bytes 589832 | tf_op jit(solution)/shard_map/ppermute | solution.py:823
  40.2 15.6 %collective-permute-start.12 = (bf16[128,768]{1,0:T(8,128)(2,1)S(1)}, bf16[128,768]{1,0:T(8,128)(2,1)S(1)}, u32[]{:S(2)}, u32[]{:S(2)}) collective-permute-start(bf16[128,768]{1,0:T(8,128)(2,1)S(1)} %get-tuple-element.168), channel_id=1, source_target_pairs={{0,0},{1,16},{2,8},{3,24},{4,4},{5,20},{6,12},{7,28},{8,2},{9,18},... | collective-permute-start | bytes 589832 | tf_op jit(solution)/shard_map/ppermute | solution.py:823
  59.5 11.2 %collective-permute-start.15 = (bf16[256,768]{1,0:T(8,128)(2,1)S(1)}, bf16[256,768]{1,0:T(8,128)(2,1)S(1)}, u32[]{:S(2)}, u32[]{:S(2)}) collective-permute-start(bf16[256,768]{1,0:T(8,128)(2,1)S(1)} %tail_kernel.4), channel_id=1, source_target_pairs={{0,2},{1,3},{2,0},{3,1},{4,6},{5,7},{6,4},{7,5},{8,10},{9,11},{10,... | collective-permute-start | bytes 1179656 | tf_op jit(solution)/shard_map/ppermute | solution.py:66
  59.5 12.0 %collective-permute-start.19 = (bf16[2,96,768]{2,1,0:T(8,128)(2,1)S(1)}, bf16[2,96,768]{2,1,0:T(8,128)(2,1)S(1)}, u32[]{:S(2)}, u32[]{:S(2)}) collective-permute-start(bf16[2,96,768]{2,1,0:T(8,128)(2,1)S(1)} %collective-permute-done.11.y_ref), channel_id=1, source_target_pairs={{0,4},{4,0},{8,12},{12,8},{16,20},{20,16},{24,28},{28,24},{1,5},{5... | collective-permute-start | bytes 884744 | tf_op jit(solution)/shard_map/ppermute | solution.py:71
  60.9 11.5 %collective-permute-start.20 = (bf16[2,96,768]{2,1,0:T(8,128)(2,1)S(1)}, bf16[2,96,768]{2,1,0:T(8,128)(2,1)S(1)}, u32[]{:S(2)}, u32[]{:S(2)}) collective-permute-start(bf16[2,96,768]{2,1,0:T(8,128)(2,1)S(1)} %collective-permute-done.11.y_ref), channel_id=1, source_target_pairs={{0,1},{1,0},{2,3},{3,2},{4,5},{5,4},{6,7},{7,6},{8,9},{9,8},{10,11... | collective-permute-start | bytes 884744 | tf_op jit(solution)/shard_map/ppermute | solution.py:66
  60.9 11.5 %collective-permute-start.18 = (bf16[192,768]{1,0:T(8,128)(2,1)S(1)}, bf16[192,768]{1,0:T(8,128)(2,1)S(1)}, u32[]{:S(2)}, u32[]{:S(2)}) collective-permute-start(bf16[192,768]{1,0:T(8,128)(2,1)S(1)} %get-tuple-element.177), channel_id=1, source_target_pairs={{0,1},{1,0},{2,3},{3,2},{4,5},{5,4},{6,7},{7,6},{8,9},{9,8},{10,11... | collective-permute-start | bytes 884744 | tf_op jit(solution)/shard_map/ppermute | solution.py:66
  89.5 11.2 %collective-permute-start.25 = (bf16[256,768]{1,0:T(8,128)(2,1)S(1)}, bf16[256,768]{1,0:T(8,128)(2,1)S(1)}, u32[]{:S(2)}, u32[]{:S(2)}) collective-permute-start(bf16[256,768]{1,0:T(8,128)(2,1)S(1)} %tail_kernel.5), channel_id=1, source_target_pairs={{0,2},{1,3},{2,0},{3,1},{4,6},{5,7},{6,4},{7,5},{8,10},{9,11},{10,... | collective-permute-start | bytes 1179656 | tf_op jit(solution)/shard_map/ppermute | solution.py:66
  102.1 11.5 %collective-permute-start.27 = (bf16[256,768]{1,0:T(8,128)(2,1)S(1)}, bf16[256,768]{1,0:T(8,128)(2,1)S(1)}, u32[]{:S(2)}, u32[]{:S(2)}) collective-permute-start(bf16[256,768]{1,0:T(8,128)(2,1)S(1)} %get-tuple-element.188.own_ref), channel_id=1, source_target_pairs={{0,2},{1,3},{2,0},{3,1},{4,6},{5,7},{6,4},{7,5},{8,10},{9,11},{10,... | collective-permute-start | bytes 1179656 | tf_op jit(solution)/shard_map/ppermute | solution.py:66
  119.4 15.4 %collective-permute-start.33 = (bf16[4,96,768]{2,1,0:T(8,128)(2,1)S(1)}, bf16[4,96,768]{2,1,0:T(8,128)(2,1)S(1)}, u32[]{:S(2)}, u32[]{:S(2)}) collective-permute-start(bf16[4,96,768]{2,1,0:T(8,128)(2,1)S(1)} %get-tuple-element.196), channel_id=1, source_target_pairs={{0,4},{4,0},{8,12},{12,8},{16,20},{20,16},{24,28},{28,24},{1,5},{5... | collective-permute-start | bytes 1769480 | tf_op jit(solution)/shard_map/ppermute | solution.py:71
  146.7 18.6 %collective-permute-start.38 = (bf16[20,24,768]{2,1,0:T(8,128)(2,1)S(1)}, bf16[20,24,768]{2,1,0:T(8,128)(2,1)S(1)}, u32[]{:S(2)}, u32[]{:S(2)}) collective-permute-start(bf16[20,24,768]{2,1,0:T(8,128)(2,1)S(1)} %get-tuple-element.223), channel_id=1, source_target_pairs={{0,4},{4,0},{8,12},{12,8},{16,20},{20,16},{24,28},{28,24},{1,5},{5... | collective-permute-start | bytes 2211848 | tf_op jit(solution)/shard_map/ppermute | solution.py:71
  148.2 15.3 %collective-permute-start.37 = (bf16[1,96,768]{2,1,0:T(8,128)(2,1)S(1)}, bf16[1,96,768]{2,1,0:T(8,128)(2,1)S(1)}, u32[]{:S(2)}, u32[]{:S(2)}) collective-permute-start(bf16[1,96,768]{2,1,0:T(8,128)(2,1)S(1)} %get-tuple-element.221), channel_id=1, source_target_pairs={{0,16},{4,20},{8,24},{12,28},{16,0},{20,4},{24,8},{28,12},{1,17},{... | collective-permute-start | bytes 442376 | tf_op jit(solution)/shard_map/ppermute | solution.py:71
  169.6 13.5 %collective-permute-start.41 = (bf16[10,24,768]{2,1,0:T(8,128)(2,1)S(1)}, bf16[10,24,768]{2,1,0:T(8,128)(2,1)S(1)}, u32[]{:S(2)}, u32[]{:S(2)}) collective-permute-start(bf16[10,24,768]{2,1,0:T(8,128)(2,1)S(1)} %get-tuple-element.235), channel_id=1, source_target_pairs={{0,8},{4,12},{8,0},{12,4},{16,24},{20,28},{24,16},{28,20},{1,9},{5... | collective-permute-start | bytes 1105928 | tf_op jit(solution)/shard_map/ppermute | solution.py:71
  175.1 14.9 %collective-permute-start.45 = (bf16[12,24,768]{2,1,0:T(8,128)(2,1)S(1)}, bf16[12,24,768]{2,1,0:T(8,128)(2,1)S(1)}, u32[]{:S(2)}, u32[]{:S(2)}) collective-permute-start(bf16[12,24,768]{2,1,0:T(8,128)(2,1)S(1)} %get-tuple-element.231), channel_id=1, source_target_pairs={{0,4},{4,0},{8,12},{12,8},{16,20},{20,16},{24,28},{28,24},{1,5},{5... | collective-permute-start | bytes 1327112 | tf_op jit(solution)/shard_map/ppermute | solution.py:71
  186.6 12.6 %collective-permute-start.47 = (bf16[2,96,768]{2,1,0:T(8,128)(2,1)S(1)}, bf16[2,96,768]{2,1,0:T(8,128)(2,1)S(1)}, u32[]{:S(2)}, u32[]{:S(2)}) collective-permute-start(bf16[2,96,768]{2,1,0:T(8,128)(2,1)S(1)} %get-tuple-element.251.refs_3_), channel_id=1, source_target_pairs={{0,8},{4,12},{8,0},{12,4},{16,24},{20,28},{24,16},{28,20},{1,9},{5... | collective-permute-start | bytes 884744 | tf_op jit(solution)/shard_map/ppermute | solution.py:71
  188.3 30.6 %collective-permute-start.44 = (bf16[2,128,768]{2,1,0:T(8,128)(2,1)S(1)}, bf16[2,128,768]{2,1,0:T(8,128)(2,1)S(1)}, u32[]{:S(2)}, u32[]{:S(2)}) collective-permute-start(bf16[2,128,768]{2,1,0:T(8,128)(2,1)S(1)} %get-tuple-element.240), channel_id=1, source_target_pairs={{4,0},{20,1},{12,2},{28,3},{0,4},{16,5},{8,6},{24,7},{6,8},{22,9},... | collective-permute-start | bytes 1179656 | tf_op jit(solution)/shard_map/ppermute | solution.py:827
  190.7 18.7 %collective-permute-start.48 = (bf16[6,24,768]{2,1,0:T(8,128)(2,1)S(1)}, bf16[6,24,768]{2,1,0:T(8,128)(2,1)S(1)}, u32[]{:S(2)}, u32[]{:S(2)}) collective-permute-start(bf16[6,24,768]{2,1,0:T(8,128)(2,1)S(1)} %get-tuple-element.246), channel_id=1, source_target_pairs={{0,8},{4,12},{8,0},{12,4},{16,24},{20,28},{24,16},{28,20},{1,9},{5... | collective-permute-start | bytes 663560 | tf_op jit(solution)/shard_map/ppermute | solution.py:71
  199.8 31.1 %collective-permute-start.54 = (bf16[4,96,768]{2,1,0:T(8,128)(2,1)S(1)}, bf16[4,96,768]{2,1,0:T(8,128)(2,1)S(1)}, u32[]{:S(2)}, u32[]{:S(2)}) collective-permute-start(bf16[4,96,768]{2,1,0:T(8,128)(2,1)S(1)} %get-tuple-element.252.refs_3_), channel_id=1, source_target_pairs={{0,4},{4,0},{8,12},{12,8},{16,20},{20,16},{24,28},{28,24},{1,5},{5... | collective-permute-start | bytes 1769480 | tf_op jit(solution)/shard_map/ppermute | solution.py:71
  201.3 14.2 %collective-permute-start.50 = (bf16[2,24,768]{2,1,0:T(8,128)(2,1)S(1)}, bf16[2,24,768]{2,1,0:T(8,128)(2,1)S(1)}, u32[]{:S(2)}, u32[]{:S(2)}) collective-permute-start(bf16[2,24,768]{2,1,0:T(8,128)(2,1)S(1)} %get-tuple-element.258), channel_id=1, source_target_pairs={{0,2},{1,3},{2,0},{3,1},{4,6},{5,7},{6,4},{7,5},{8,10},{9,11},{10,... | collective-permute-start | bytes 221192 | tf_op jit(solution)/shard_map/ppermute | solution.py:66
  216.9 14.0 %collective-permute-start.53 = (bf16[6,24,768]{2,1,0:T(8,128)(2,1)S(1)}, bf16[6,24,768]{2,1,0:T(8,128)(2,1)S(1)}, u32[]{:S(2)}, u32[]{:S(2)}) collective-permute-start(bf16[6,24,768]{2,1,0:T(8,128)(2,1)S(1)} %get-tuple-element.264.refs_0_), channel_id=1, source_target_pairs={{0,16},{4,20},{8,24},{12,28},{16,0},{20,4},{24,8},{28,12},{1,17},{... | collective-permute-start | bytes 663560 | tf_op jit(solution)/shard_map/ppermute | solution.py:71
  233.0 14.0 %collective-permute-start.58 = (bf16[11,24,768]{2,1,0:T(8,128)(2,1)S(1)}, bf16[11,24,768]{2,1,0:T(8,128)(2,1)S(1)}, u32[]{:S(2)}, u32[]{:S(2)}) collective-permute-start(bf16[11,24,768]{2,1,0:T(8,128)(2,1)S(1)} %get-tuple-element.271.refs_0_), channel_id=1, source_target_pairs={{0,8},{4,12},{8,0},{12,4},{16,24},{20,28},{24,16},{28,20},{1,9},{5... | collective-permute-start | bytes 1216520 | tf_op jit(solution)/shard_map/ppermute | solution.py:71
  247.6 20.2 %collective-permute-start.61 = (bf16[21,24,768]{2,1,0:T(8,128)(2,1)S(1)}, bf16[21,24,768]{2,1,0:T(8,128)(2,1)S(1)}, u32[]{:S(2)}, u32[]{:S(2)}) collective-permute-start(bf16[21,24,768]{2,1,0:T(8,128)(2,1)S(1)} %get-tuple-element.275.refs_1_), channel_id=1, source_target_pairs={{0,4},{4,0},{8,12},{12,8},{16,20},{20,16},{24,28},{28,24},{1,5},{5... | collective-permute-start | bytes 2322440 | tf_op jit(solution)/shard_map/ppermute | solution.py:71
  257.6 18.6 %collective-permute-start.62 = (bf16[12,24,768]{2,1,0:T(8,128)(2,1)S(1)}, bf16[12,24,768]{2,1,0:T(8,128)(2,1)S(1)}, u32[]{:S(2)}, u32[]{:S(2)}) collective-permute-start(bf16[12,24,768]{2,1,0:T(8,128)(2,1)S(1)} %qkv_low.1.refs_2_), channel_id=1, source_target_pairs={{0,4},{4,0},{8,12},{12,8},{16,20},{20,16},{24,28},{28,24},{1,5},{5... | collective-permute-start | bytes 1327112 | tf_op jit(solution)/shard_map/ppermute | solution.py:71
  258.4 17.6 %collective-permute-start.43 = (bf16[2,128,768]{2,1,0:T(8,128)(2,1)S(1)}, bf16[2,128,768]{2,1,0:T(8,128)(2,1)S(1)}, u32[]{:S(2)}, u32[]{:S(2)}) collective-permute-start(bf16[2,128,768]{2,1,0:T(8,128)(2,1)S(1)} %get-tuple-element.239), channel_id=1, source_target_pairs={{0,0},{16,1},{8,2},{24,3},{4,4},{20,5},{12,6},{28,7},{2,8},{18,9},... | collective-permute-start | bytes 1179656 | tf_op jit(solution)/shard_map/ppermute | solution.py:826
  (37 other events, 243.5 us)
